TPU v7x, 512 devices: a whole 4x4x16 slice. The times are simulated.
512 devices in a mesh: lev: 32 (over x_lo, z), mem: 16 (over x_hi, y, core).
Axes of the slice: x: 4 (x_hi: 2, x_lo: 2; x = x_hi * 2 + x_lo), y: 4, z: 16, core: 2. Of those that a mesh axis runs over, the one named last changes fastest.
Arguments:
- control: bfloat16 [32, 5, 128, 4096], P('mem', None, 'lev'), may hold values from -6 to 6
- static_control_vector: bfloat16 [5, 128, 4096], P(None, None, 'lev'), may hold values from -6 to 6
- perturb: bfloat16 [32, 5, 128, 4096], P('mem', None, None, 'lev'), may hold values from -6 to 6
- tiles: bfloat16 [4, 64, 64], replicated, may hold values from -0.375 to 0.375
- block_offset: int32 [64, 4], replicated, may hold values from -8 to 8
- vert: bfloat16 [5, 128, 128], replicated, may hold values from -0.5 to 0.5
- static_vertical_root: bfloat16 [5, 128, 128], replicated, may hold values from -0.5 to 0.5
- obs_index: int32 [524288], P(('lev', 'mem')), may hold values from 0 to 5119
- obs_value: float32 [524288], P(('lev', 'mem')), may hold values from -6 to 6
- obs_sigma: float32 [524288], P(('lev', 'mem')), may hold values from 0.3 to 1
- huber_mask: int32 [524288], P(('lev', 'mem')), may hold values 0 or 1
Outputs:
- control_out: bfloat16 [32, 5, 128, 4096], P('mem', None, 'lev')
- static_out: bfloat16 [5, 128, 4096], P(None, None, 'lev')
Inputs may be any that keep to these rules, and one draw needn't show every extreme that they name: `obs_index`: indices count in the block held by the observation's own device: 5 variables, 128 / 16 levels, 128 columns, in that order. `block_offset`: source blocks wrap around the window.
All inputs are finite; a program needn't handle non-finite values. No bound on the sum of `huber_mask` on one device may be relied on, other than what follows from the above.
Results may differ from a plain program's by a relative error of at most 0.0057.
Values may be sent and summed in bfloat16 or wider, within the bound.
No kernel may reach another device: no remote copies, remote signals or barrier semaphores. Data moves between devices by JAX's collectives and lax.ppermute only.
A program may use at most 64 MiB of HBM per device.

v0:
```python
import math

import jax
import jax.numpy as jnp
from jax import lax
from jax.sharding import PartitionSpec as P

ITERS = 2


ENS_W = 0.85
STATIC_WEIGHT = 0.5
TAU = 0.5
HUBER_LOW = 0.3


def selectors(block_offset):
    count = block_offset.shape[0]
    blocks = jnp.arange(count, dtype=jnp.int32)
    source = (blocks[:, None] + block_offset) % count
    return (source.T[:, :, None] == blocks[None, None, :]).astype(jnp.bfloat16)


def horizontal(field, tiles, picks):
    count = picks.shape[1]
    width = tiles.shape[1]
    shaped = field.reshape(field.shape[:-1] + (count, width))
    total = None
    for slot in range(tiles.shape[0]):
        moved = jnp.einsum(
            "bj,...jc->...bc", picks[slot], shaped, preferred_element_type=jnp.float32
        ).astype(jnp.bfloat16)
        term = jnp.einsum("...bc,cd->...bd", moved, tiles[slot], preferred_element_type=jnp.float32)
        total = term if total is None else total + term
    return total.reshape(field.shape).astype(jnp.bfloat16)


def horizontal_adjoint(field, tiles, picks):
    count = picks.shape[1]
    width = tiles.shape[1]
    shaped = field.reshape(field.shape[:-1] + (count, width))
    total = None
    for slot in range(tiles.shape[0]):
        term = jnp.einsum(
            "...bc,dc->...bd", shaped, tiles[slot], preferred_element_type=jnp.float32
        )
        moved = jnp.einsum(
            "bj,...bd->...jd",
            picks[slot].astype(jnp.float32),
            term,
            precision=lax.Precision.HIGHEST,
        )
        total = moved if total is None else total + moved
    return total.reshape(field.shape)


def observe(block, obs_index, obs_value, precision_obs):
    flat = block.reshape(-1)
    seen = flat[obs_index]
    resid = precision_obs * (seen - obs_value)
    return jnp.zeros_like(flat).at[obs_index].add(resid).reshape(block.shape)


def on_device(
    control,
    static_control_vector,
    perturb,
    tiles,
    block_offset,
    vert,
    static_vertical_root,
    obs_index,
    obs_value,
    obs_sigma,
    huber_mask,
):
    picks = selectors(block_offset)
    members_all = control.shape[0] * lax.axis_size("mem")
    ens_gain = ENS_W / math.sqrt(members_all)
    level_rows = static_control_vector.shape[1] // lax.axis_size("mem")
    first_level = lax.axis_index("mem") * level_rows
    weights = jnp.where(huber_mask == 1, jnp.float32(1.0), jnp.float32(HUBER_LOW))
    precision_obs = weights / (obs_sigma * obs_sigma)
    vertical_forward = vert.astype(jnp.float32)
    static_forward = static_vertical_root.astype(jnp.float32)
    for turn in range(ITERS):
        local = horizontal(control, tiles, picks)
        columns = lax.all_to_all(local, "lev", split_axis=3, concat_axis=2, tiled=True)
        vertical = jnp.einsum("vlk,mvkc->mvlc", vert, columns, preferred_element_type=jnp.float32)
        partial_value = jnp.sum(vertical * perturb.astype(jnp.float32), axis=0)
        static_portion = jnp.einsum(
            "tbu,tuo->tbo",
            static_vertical_root,
            static_control_vector,
            preferred_element_type=jnp.float32,
        )
        ens = lax.psum(partial_value, "mem")
        increment = ens_gain * ens + STATIC_WEIGHT * static_portion
        own_block = lax.dynamic_slice_in_dim(increment, first_level, level_rows, 1)
        grad_block = observe(own_block, obs_index, obs_value, precision_obs)
        placed = lax.dynamic_update_slice_in_dim(
            jnp.zeros_like(increment), grad_block, first_level, 1
        )
        gradient_field_total = lax.psum(placed, "mem")
        static_gradient = static_control_vector.astype(jnp.float32) + STATIC_WEIGHT * jnp.einsum(
            "otn,ote->one", static_forward, gradient_field_total, precision=lax.Precision.HIGHEST
        )
        weighted_innovations = (ens_gain * gradient_field_total)[None] * perturb.astype(jnp.float32)
        backward_field = jnp.einsum(
            "vkl,mvkc->mvlc",
            vertical_forward,
            weighted_innovations,
            precision=lax.Precision.HIGHEST,
        ).astype(jnp.bfloat16)
        levels = lax.all_to_all(backward_field, "lev", split_axis=2, concat_axis=3, tiled=True)
        adjoint = horizontal_adjoint(levels, tiles, picks)
        current = control.astype(jnp.float32)
        control = (current - TAU * (current + adjoint)).astype(jnp.bfloat16)
        static_control_vector = (
            static_control_vector.astype(jnp.float32) - TAU * static_gradient
        ).astype(jnp.bfloat16)
    return (control, static_control_vector)


def solution(mesh):
    placed = (
        P("mem", None, "lev", None),
        P(None, None, "lev"),
        P("mem", None, None, "lev"),
        P(),
        P(),
        P(),
        P(),
        P(("lev", "mem")),
        P(("lev", "mem")),
        P(("lev", "mem")),
        P(("lev", "mem")),
    )
    return jax.shard_map(
        on_device,
        mesh=mesh,
        in_specs=placed,
        out_specs=(P("mem", None, "lev", None), P(None, None, "lev")),
        check_vma=False,
    )
```

profile of v0, /device:TPU:4, one launch (start us, length us, event | category | flops | bytes accessed | tf_op | source)
XLA Modules:
  0.0 919.5 jit_solution(7885680321525011483)
XLA Ops:
  8.0 1.6 reshape.43
  9.6 1.2 fusion.5
  12.5 9.9 %copy.161 = bf16[2,5,4,64,64]{1,2,0,4,3:T(4,128)(2,1)} copy(bf16[2,5,4,64,64]{4,3,2,1,0:T(8,128)(2,1)S(1)} %fusion.2) | data formatting | bytes 655360 | tf_op jit(solution)/shard_map/convert_element_type | solution.py:35
  22.3 13.3 %reshape.102 = bf16[32,2,2560]{2,1,0:T(2,128)(2,1)} reshape(bf16[4096,2,4,5]{3,2,1,0:T(4,128)(2,1)} %bitcast.255) | data formatting | bytes 655360
  35.6 16.1 %all-to-all-start = ((bf16[32,2,2560]{2,1,0:T(2,128)(2,1)}), bf16[32,2,2560]{2,1,0:T(2,128)(2,1)S(1)}, u32[]{:S(2)}, u32[]{:S(2)}) async-start(bf16[32,2,2560]{2,1,0:T(2,128)(2,1)} %reshape.102), calls=%async_computation | async-start | bytes 655360 | tf_op jit(solution)/shard_map/all_to_all | solution.py:88
  52.0 24.5 %all-to-all-done = bf16[32,2,2560]{2,1,0:T(2,128)(2,1)S(1)} async-done(((bf16[32,2,2560]{2,1,0:T(2,128)(2,1)}), bf16[32,2,2560]{2,1,0:T(2,128)(2,1)S(1)}, u32[]{:S(2)}, u32[]{:S(2)}) %all-to-all-start) | async-done | bytes 327712 | tf_op jit(solution)/shard_map/all_to_all | solution.py:88
  76.5 19.2 %reshape.103 = bf16[4096,2,4,5]{3,2,1,0:T(4,128)(2,1)} reshape(bf16[32,2,2560]{2,1,0:T(2,128)(2,1)S(1)} %all-to-all-done) | data formatting | bytes 655360
  95.7 11.4 %copy.89 = bf16[2,5,4,32,128]{4,2,3,1,0:T(4,128)(2,1)S(1)} copy(bf16[2,5,4,32,128]{1,2,0,4,3:T(4,128)(2,1)} %bitcast.256) | data formatting | bytes 655360 | tf_op jit(solution)/shard_map/all_to_all | solution.py:88
  108.7 143.3 %all-reduce.5.cloned.1.call-done = f32[5,128,128]{2,1,0:T(8,128)} async-done(((f32[5,128,128]{2,1,0:T(8,128)}), f32[5,128,128]{2,1,0:T(8,128)}) %all-reduce.5.cloned.1.call-update) | async-done | bytes 327696 | tf_op jit(solution)/shard_map/psum | solution.py:97
  252.7 6.2 gather_fusion
  258.9 5.9 scatter_custom_fusion
  265.7 151.5 %all-reduce.7.cloned.1.call-done = f32[5,128,128]{2,1,0:T(8,128)} async-done(((f32[5,128,128]{2,1,0:T(8,128)}), f32[5,128,128]{2,1,0:T(8,128)}) %all-reduce.7.cloned.1.call-update) | async-done | bytes 327696 | tf_op jit(solution)/shard_map/psum | solution.py:104
  417.2 1.0 broadcast_multiply_fusion
  419.6 36.8 %all_to_all.66 = bf16[2,5,128,128]{3,0,1,2:T(2,128)(2,1)S(1)} all-to-all(bf16[2,5,128,128]{3,0,1,2:T(2,128)(2,1)S(1)} %copy.95), channel_id=1, replica_groups=mesh['lev'=32,'mem'=16] {'lev'}, dimensions={2} | all-to-all | bytes 655360 | tf_op jit(solution)/shard_map/all_to_all | solution.py:115
  462.1 1.8 fusion.1
  463.9 1.7 copy.102
  468.1 1.8 convolution_add_fusion.2
  469.8 2.0 convolution_add_fusion.1
  471.9 1.6 fusion.3
  473.4 11.7 %copy.163 = bf16[2,5,4,64,64]{1,2,0,4,3:T(4,128)(2,1)} copy(bf16[2,5,4,64,64]{4,3,2,1,0:T(8,128)(2,1)} %fusion.3) | data formatting | bytes 655360 | tf_op jit(solution)/shard_map/convert_element_type | solution.py:35
  485.1 13.2 %reshape.104 = bf16[32,2,2560]{2,1,0:T(2,128)(2,1)} reshape(bf16[4096,2,4,5]{3,2,1,0:T(4,128)(2,1)} %bitcast.257) | data formatting | bytes 655360
  498.3 3.9 all-to-all-start.2
  502.7 21.9 %all-to-all-done.2 = bf16[32,2,2560]{2,1,0:T(2,128)(2,1)S(1)} async-done(((bf16[32,2,2560]{2,1,0:T(2,128)(2,1)}), bf16[32,2,2560]{2,1,0:T(2,128)(2,1)S(1)}, u32[]{:S(2)}, u32[]{:S(2)}) %all-to-all-start.2) | async-done | bytes 327712 | tf_op jit(solution)/shard_map/all_to_all | solution.py:88
  524.5 19.2 %reshape.105 = bf16[4096,2,4,5]{3,2,1,0:T(4,128)(2,1)} reshape(bf16[32,2,2560]{2,1,0:T(2,128)(2,1)S(1)} %all-to-all-done.2) | data formatting | bytes 655360
  543.7 11.4 %copy.112 = bf16[2,5,4,32,128]{4,2,3,1,0:T(4,128)(2,1)S(1)} copy(bf16[2,5,4,32,128]{1,2,0,4,3:T(4,128)(2,1)} %bitcast.258) | data formatting | bytes 655360 | tf_op jit(solution)/shard_map/all_to_all | solution.py:88
  557.1 142.3 %all-reduce.9.cloned.1.call-done = f32[5,128,128]{2,1,0:T(8,128)} async-done(((f32[5,128,128]{2,1,0:T(8,128)}), f32[5,128,128]{2,1,0:T(8,128)}) %all-reduce.9.cloned.1.call-update) | async-done | bytes 327696 | tf_op jit(solution)/shard_map/psum | solution.py:97
  700.2 6.1 gather_fusion.1
  706.3 6.1 scatter_custom_fusion.1
  713.2 151.5 %all-reduce.11.cloned.1.call-done = f32[5,128,128]{2,1,0:T(8,128)} async-done(((f32[5,128,128]{2,1,0:T(8,128)}), f32[5,128,128]{2,1,0:T(8,128)}) %all-reduce.11.cloned.1.call-update) | async-done | bytes 327696 | tf_op jit(solution)/shard_map/psum | solution.py:104
  866.4 1.3 copy.120
  867.6 13.5 %all-to-all-start.3 = ((bf16[2,5,128,128]{3,0,1,2:T(2,128)(2,1)}), bf16[2,5,128,128]{3,0,1,2:T(2,128)(2,1)S(1)}, u32[]{:S(2)}, u32[]{:S(2)}) async-start(bf16[2,5,128,128]{3,0,1,2:T(2,128)(2,1)} %copy.120), calls=%async_computation.3 | async-start | bytes 655360 | tf_op jit(solution)/shard_map/all_to_all | solution.py:115
  882.4 22.2 %all-to-all-done.3 = bf16[2,5,128,128]{3,0,1,2:T(2,128)(2,1)S(1)} async-done(((bf16[2,5,128,128]{3,0,1,2:T(2,128)(2,1)}), bf16[2,5,128,128]{3,0,1,2:T(2,128)(2,1)S(1)}, u32[]{:S(2)}, u32[]{:S(2)}) %all-to-all-start.3) | async-done | bytes 327712 | tf_op jit(solution)/shard_map/all_to_all | solution.py:115
  (97 shorter events, 30.1 us)
Async XLA Ops:
  7.2 100.0 %copy-start = (bf16[5,128,128]{2,1,0:T(8,128)(2,1)S(1)}, bf16[5,128,128]{2,1,0:T(8,128)(2,1)}, u32[]{:S(2)}) copy-start(bf16[5,128,128]{2,1,0:T(8,128)(2,1)} %param.16) | copy-start | bytes 491524
  8.0 2.8 copy-start.7
  22.3 29.4 %copy-start.9 = (bf16[2,5,128,128]{3,2,1,0:T(8,128)(2,1)S(1)}, bf16[2,5,128,128]{3,2,1,0:T(8,128)(2,1)}, u32[]{:S(2)}) copy-start(bf16[2,5,128,128]{3,2,1,0:T(8,128)(2,1)} %param.13) | copy-start | bytes 983044
  35.6 40.9 %all-to-all-start = ((bf16[32,2,2560]{2,1,0:T(2,128)(2,1)}), bf16[32,2,2560]{2,1,0:T(2,128)(2,1)S(1)}, u32[]{:S(2)}, u32[]{:S(2)}) async-start(bf16[32,2,2560]{2,1,0:T(2,128)(2,1)} %reshape.102), calls=%async_computation | async-start | bytes 655360 | tf_op jit(solution)/shard_map/all_to_all | solution.py:88
  51.7 200.2 %all-reduce.5.cloned.1.call-start = ((), (), s32[]{:S(2)}) async-start(), calls=%async_computation.4 | async-start | bytes 655360 | tf_op jit(solution)/shard_map/psum | solution.py:97
  107.1 1.3 copy-start.13
  107.1 1.4 copy-start.1
  107.1 1.4 copy-start.8
  108.4 308.8 %all-reduce.7.cloned.1.call-start = ((), (), s32[]{:S(2)}) async-start(), calls=%async_computation.5 | async-start | bytes 655360 | tf_op jit(solution)/shard_map/psum | solution.py:104
  108.5 150.5 %copy-start.14 = (s32[1024]{0:T(1024)}, s32[1024]{0:T(1024)S(1)}, u32[]{:S(2)}) copy-start(s32[1024]{0:T(1024)S(1)} %get-tuple-element.11) | copy-start | bytes 12292
  252.7 6.2 copy-start.10
  252.7 6.2 copy-start.11
  252.7 6.2 copy-start.12
  264.9 0.7 copy-start.6
  465.6 1.0 copy-start.4
  498.3 26.2 %all-to-all-start.2 = ((bf16[32,2,2560]{2,1,0:T(2,128)(2,1)}), bf16[32,2,2560]{2,1,0:T(2,128)(2,1)S(1)}, u32[]{:S(2)}, u32[]{:S(2)}) async-start(bf16[32,2,2560]{2,1,0:T(2,128)(2,1)} %reshape.104), calls=%async_computation.2 | async-start | bytes 655360 | tf_op jit(solution)/shard_map/all_to_all | solution.py:88
  502.2 197.2 %all-reduce.9.cloned.1.call-start = ((), (), s32[]{:S(2)}) async-start(), calls=%async_computation.6 | async-start | bytes 655360 | tf_op jit(solution)/shard_map/psum | solution.py:97
  555.1 1.3 copy-start.2
  556.4 308.4 %all-reduce.11.cloned.1.call-start = ((), (), s32[]{:S(2)}) async-start(), calls=%async_computation.7 | async-start | bytes 655360 | tf_op jit(solution)/shard_map/psum | solution.py:104
  712.5 0.7 copy-start.5
  865.9 15.2 %copy-start.3 = (f32[5,128,128]{2,1,0:T(8,128)S(1)}, f32[5,128,128]{2,1,0:T(8,128)}, u32[]{:S(2)}) copy-start(f32[5,128,128]{2,1,0:T(8,128)} %all-reduce.11.cloned.1.call-done) | copy-start | bytes 983044
  867.6 37.0 %all-to-all-start.3 = ((bf16[2,5,128,128]{3,0,1,2:T(2,128)(2,1)}), bf16[2,5,128,128]{3,0,1,2:T(2,128)(2,1)S(1)}, u32[]{:S(2)}, u32[]{:S(2)}) async-start(bf16[2,5,128,128]{3,0,1,2:T(2,128)(2,1)} %copy.120), calls=%async_computation.3 | async-start | bytes 655360 | tf_op jit(solution)/shard_map/all_to_all | solution.py:115
Sparse Core Ops, SparseCore 0:
  108.5 143.3 all-reduce.4
  265.8 151.3 all-reduce.6
  556.5 142.9 all-reduce.8
  713.3 151.3 all-reduce.10
where the time goes:
time: 922 us; the launch traced here: 920 us
  waiting for transfers between devices  657 us (71%)
  local copies, waits for them, and re-layouts  135 us (15%)
  blocking collectives  36.8 us (4%)
  starting transfers between devices  33.9 us (4%)
  matrix products  24.7 us (3%)
  other arithmetic  17.5 us (2%)
  between operations  14.4 us (2%)
    psum x2, waiting for transfers between devices, on_device(): gradient_field_total = lax.psum(placed, 'mem')  303 us
    psum x2, waiting for transfers between devices, on_device(): ens = lax.psum(partial_value, 'mem')  286 us
    unnamed x37, local copies, waits for them, and re-layouts  67.9 us
    all_to_all x2, waiting for transfers between devices, on_device(): lax.all_to_all(local, 'lev', split_axis=3, concat_axis=2, tiled=True)  46.4 us
    all_to_all x1, blocking collectives, on_device(): lax.all_to_all(backward_field, 'lev', split_axis=2, concat_axis=3, tiled=...  36.8 us
    all_to_all x2, local copies, waits for them, and re-layouts, on_device(): lax.all_to_all(local, 'lev', split_axis=3, concat_axis=2, tiled=True)  22.9 us
    all_to_all x1, waiting for transfers between devices, on_device(): lax.all_to_all(backward_field, 'lev', split_axis=2, concat_axis=3, tiled=...  22.2 us
    convert_element_type x2, local copies, waits for them, and re-layouts, horizontal(): return total.reshape(field.shape).astype(jnp.bfloat16)  21.6 us
  transfers between devices with their start and end apart: 7, of which 7 were waited for; matrix products, arithmetic and copies ran while one was open for 0% of the time, Pallas kernels for 0%

commit v1 on v0

v1 whole, which is shorter than its diff:
```python
import functools
import math

import jax
import jax.numpy as jnp
from jax import lax
from jax.experimental import pallas as pl
from jax.experimental.pallas import tpu as pltpu
from jax.sharding import PartitionSpec as P

ITERS = 2

ENS_W = 0.85
STATIC_WEIGHT = 0.5
TAU = 0.5
HUBER_LOW = 0.3

F32 = jnp.float32
BF16 = jnp.bfloat16
LANES = 128
HALF = 64


def call(body, out_shape, scratch=()):
    return pl.pallas_call(body, out_shape=out_shape, scratch_shapes=list(scratch), name=body.__name__)


def dot(a, b, dims=((1,), (0,))):
    return lax.dot_general(a, b, (dims, ((), ())), preferred_element_type=F32)


def spread(load, pick_ref, weight_ref, gathered):
    rows = gathered.shape[0] // 32
    lane = lax.broadcasted_iota(jnp.int32, (32, LANES), 1)
    pick = pick_ref[...]
    for first in range(0, rows, 2):
        columns = []
        for r in (first, first + 1):
            x = load(r)
            low = jnp.where(lane < HALF, x, 0.0)
            columns.append(jnp.concatenate([low, x - low], axis=0).astype(BF16))
        moved = dot(pick, jnp.concatenate(columns, axis=1)).astype(BF16)
        for i in range(2):
            for a in range(8):
                gathered[pl.ds((first + i) * 32, 32), pl.ds(a * LANES, LANES)] = moved[
                    a * 32 : a * 32 + 32, i * LANES : (i + 1) * LANES
                ]
    return dot(gathered[...], weight_ref[...])


def open_chunks(recv_ref, scratch):
    rows = recv_ref.shape[1]
    for j in range(recv_ref.shape[0]):
        scratch[pl.ds(j * rows, rows), :] = recv_ref[j].astype(F32)


def close_chunks(scratch, send_ref):
    rows = send_ref.shape[1]
    for j in range(send_ref.shape[0]):
        send_ref[j] = scratch[pl.ds(j * rows, rows), :].astype(BF16)


def forward_first(control_ref, pick_ref, weight_ref, send_ref, kept_ref, flat, gathered):
    members, variables, levels, columns = control_ref.shape
    rows = members * variables * levels
    for m in range(members):
        for v in range(variables):
            x = control_ref[m, v].astype(F32)
            for j in range(columns // LANES):
                flat[pl.ds(j * rows + (m * variables + v) * levels, levels), :] = x[:, j * LANES : (j + 1) * LANES]

    def load(r):
        x = flat[pl.ds(r, 32, stride=rows), :]
        kept_ref[r] = x.astype(BF16)
        return x

    local = spread(load, pick_ref, weight_ref, gathered)
    for r in range(rows):
        flat[pl.ds(r, 32, stride=rows), :] = local[r * 32 : r * 32 + 32]
    close_chunks(flat, send_ref)


def descend(recv_ref, kept_ref, pick_ref, weight_ref, flat, gathered):
    rows = recv_ref.shape[1]
    open_chunks(recv_ref, flat)
    adjoint = spread(lambda r: flat[pl.ds(r, 32, stride=rows), :], pick_ref, weight_ref, gathered)
    current = kept_ref[...].astype(F32).reshape(rows * 32, LANES)
    return current - TAU * (current + adjoint)


def backward_forward(
    recv_ref, kept_ref, pick_t_ref, weight_t_ref, pick_ref, weight_ref, send_ref, next_ref, flat, gathered
):
    rows = recv_ref.shape[1]
    updated = descend(recv_ref, kept_ref, pick_t_ref, weight_t_ref, flat, gathered).astype(BF16)
    next_ref[...] = updated.reshape(rows, 32, LANES)
    local = spread(lambda r: next_ref[r].astype(F32), pick_ref, weight_ref, gathered)
    for r in range(rows):
        flat[pl.ds(r, 32, stride=rows), :] = local[r * 32 : r * 32 + 32]
    close_chunks(flat, send_ref)


def backward_last(recv_ref, kept_ref, pick_t_ref, weight_t_ref, control_ref, flat, gathered):
    members, variables, levels, columns = control_ref.shape
    flat[...] = descend(recv_ref, kept_ref, pick_t_ref, weight_t_ref, flat, gathered)
    for m in range(members):
        for v in range(variables):
            start = (m * variables + v) * levels * 32
            for j in range(columns // LANES):
                control_ref[m, v, :, pl.ds(j * LANES, LANES)] = flat[pl.ds(start + j, levels, stride=32), :].astype(
                    BF16
                )


def ensemble(recv_ref, perturb_ref, vert_ref, send_ref, flat):
    members, variables = perturb_ref.shape[:2]
    rows = recv_ref.shape[1]
    levels = rows // (members * variables)
    open_chunks(recv_ref, flat)
    totals = []
    for v in range(variables):
        total = None
        for m in range(members):
            start = (m * variables + v) * levels
            x = jnp.concatenate([flat[pl.ds(start + i, 32, stride=rows), :] for i in range(levels)], axis=0)
            term = dot(vert_ref[v], x.astype(BF16), ((0,), (0,))) * perturb_ref[m, v].astype(F32)
            total = term if total is None else total + term
        totals.append(total)
    deep = send_ref.shape[1] // variables
    for d in range(send_ref.shape[0]):
        send_ref[d] = jnp.concatenate([t[d * deep : (d + 1) * deep] for t in totals], axis=0).astype(send_ref.dtype)


def observations(index_ref, value_ref, sigma_ref, mask_ref, slope_ref, shift_ref):
    cells = slope_ref.shape[0]
    weights = jnp.where(mask_ref[...] == 1, F32(1.0), F32(HUBER_LOW))
    precision = weights / (sigma_ref[...] * sigma_ref[...])
    pulled = precision * value_ref[...]
    index = index_ref[...]
    lefts, rights = [], []
    for o in range(index.shape[0]):
        at = index[o : o + 1]
        row = lax.broadcasted_iota(jnp.int32, (cells, LANES), 0) == at // LANES
        lane = lax.broadcasted_iota(jnp.int32, (LANES, LANES), 0) == at % LANES
        lefts.append(
            jnp.concatenate(
                [jnp.where(row, precision[o : o + 1], 0.0), jnp.where(row, pulled[o : o + 1], 0.0)], axis=0
            )
        )
        rights.append(jnp.where(lane, F32(1.0), F32(0.0)))
    both = lax.dot_general(
        jnp.concatenate(lefts, axis=1),
        jnp.concatenate(rights, axis=1),
        (((1,), (1,)), ((), ())),
        precision=lax.Precision.HIGHEST,
        preferred_element_type=F32,
    )
    slope_ref[...] = both[:cells]
    shift_ref[...] = both[cells:]


def gradient(gain, recv_ref, static_ref, root_ref, slope_ref, shift_ref, send_ref):
    ens = jnp.sum(recv_ref[...].astype(F32), axis=0)
    static = jnp.concatenate([dot(root_ref[v], static_ref[v]) for v in range(static_ref.shape[0])], axis=0)
    increment = gain * ens + STATIC_WEIGHT * static
    grad = (slope_ref[...] * increment - shift_ref[...]).astype(send_ref.dtype)
    for d in range(send_ref.shape[0]):
        send_ref[d] = grad


def backward(gain, recv_ref, perturb_ref, vert_ref, root_ref, static_ref, send_ref, next_ref, flat):
    members, variables, levels_all = perturb_ref.shape[:3]
    rows = send_ref.shape[1]
    levels = rows // (members * variables)
    deep = recv_ref.shape[1] // variables
    field = recv_ref[...].astype(F32)
    for v in range(variables):
        grad = field[:, v * deep : (v + 1) * deep, :].reshape(levels_all, LANES)
        for m in range(members):
            weighted = ((gain * grad) * perturb_ref[m, v].astype(F32)).astype(BF16)
            back = dot(vert_ref[v], weighted)
            start = (m * variables + v) * levels
            for i in range(levels):
                flat[pl.ds(start + i, 32, stride=rows), :] = back[i * 32 : i * 32 + 32]
        current = static_ref[v].astype(F32)
        slope = current + STATIC_WEIGHT * dot(root_ref[v], grad.astype(BF16), ((0,), (0,)))
        next_ref[v] = (current - TAU * slope).astype(BF16)
    close_chunks(flat, send_ref)


def tables(block_offset):
    count, slots = block_offset.shape
    blocks = jnp.arange(count, dtype=jnp.int32)
    source = (blocks[:, None] + block_offset) % count
    spot = (source % 2) * (count // 2) + source // 2
    by_slot = spot.reshape(count // 2, 2, slots).transpose(2, 1, 0)
    place = jnp.arange(count, dtype=jnp.int32)
    forth = by_slot.reshape(-1, 1) == place[None, :]
    back = (by_slot.reshape(slots, 1, count) == place[None, :, None]).reshape(slots * count, count)
    return forth.astype(BF16), back.astype(BF16)


def weights(tiles):
    slots, width = tiles.shape[:2]
    left = jnp.pad(tiles, ((0, 0), (0, 0), (0, width)))
    right = jnp.pad(tiles, ((0, 0), (0, 0), (width, 0)))
    both = jnp.stack([left, left, right, right], axis=1)
    return both.reshape(slots * 4 * width, 2 * width)


def on_device(
    control,
    static_control_vector,
    perturb,
    tiles,
    block_offset,
    vert,
    static_vertical_root,
    obs_index,
    obs_value,
    obs_sigma,
    huber_mask,
):
    n_lev, n_mem = lax.axis_size("lev"), lax.axis_size("mem")
    members, variables, levels, columns = control.shape
    levels_all = vert.shape[1]
    deep = levels_all // n_mem
    rows, cells = members * variables * levels, variables * deep
    gain = ENS_W / math.sqrt(members * n_mem)

    pick, pick_t = tables(block_offset)
    weight, weight_t = weights(tiles), weights(jnp.swapaxes(tiles, 1, 2))
    turned = vert.reshape(variables, levels_all, n_lev, levels).transpose(0, 3, 2, 1).reshape(vert.shape)
    own_root = lax.dynamic_slice_in_dim(static_vertical_root, lax.axis_index("mem") * deep, deep, 1)

    shape = jax.ShapeDtypeStruct
    chunks = shape((n_lev, rows, LANES), BF16)
    kept = shape((rows, n_lev, LANES), BF16)
    parts = shape((n_mem, cells, LANES), BF16)
    flat = pltpu.VMEM((n_lev * rows, LANES), F32)
    gathered = pltpu.VMEM((n_lev * rows, 8 * LANES), BF16)
    field = shape((cells, LANES), F32)

    flat_obs = lambda x: x.reshape(-1, LANES)
    slope, shift = call(observations, (field, field))(
        flat_obs(obs_index), flat_obs(obs_value), flat_obs(obs_sigma), flat_obs(huber_mask)
    )
    across = lambda x, axis: lax.all_to_all(x, axis, 0, 0, tiled=True)

    send, held = call(forward_first, (chunks, kept), (flat, gathered))(control, pick, weight)
    static = static_control_vector
    for turn in range(ITERS):
        partial = call(ensemble, parts, (flat,))(across(send, "lev"), perturb, turned)
        grad_call = functools.partial(gradient, gain)
        grad_call.__name__ = "gradient"
        grad = call(grad_call, parts)(across(partial, "mem"), static, own_root, slope, shift)
        back_call = functools.partial(backward, gain)
        back_call.__name__ = "backward"
        send, static = call(back_call, (chunks, shape(static.shape, BF16)), (flat,))(
            across(grad, "mem"), perturb, turned, static_vertical_root, static
        )
        levels_back = across(send, "lev")
        if turn + 1 < ITERS:
            send, held = call(backward_forward, (chunks, kept), (flat, gathered))(
                levels_back, held, pick_t, weight_t, pick, weight
            )
        else:
            control = call(backward_last, shape(control.shape, BF16), (flat, gathered))(
                levels_back, held, pick_t, weight_t
            )
    return (control, static)


def solution(mesh):
    placed = (
        P("mem", None, "lev", None),
        P(None, None, "lev"),
        P("mem", None, None, "lev"),
        P(),
        P(),
        P(),
        P(),
        P(("lev", "mem")),
        P(("lev", "mem")),
        P(("lev", "mem")),
        P(("lev", "mem")),
    )
    return jax.shard_map(
        on_device,
        mesh=mesh,
        in_specs=placed,
        out_specs=(P("mem", None, "lev", None), P(None, None, "lev")),
        check_vma=False,
    )
```

time: 922 us -> 213 us (0.23)
  the two profiles are of different devices: /device:TPU:4 before, /device:TPU:2 now
where the time goes in v1:
time: 213 us; the launch traced here: 212 us
  blocking collectives  96 us (45%)
  waiting for transfers between devices  49.7 us (23%)
  starting transfers between devices  28.7 us (13%)
  Pallas kernels  28 us (13%)
  local copies, waits for them, and re-layouts  6.47 us (3%)
  other arithmetic  2.26 us (1%)
    all_to_all x5, blocking collectives, on_device(): across = lambda x, axis: lax.all_to_all(x, axis, 0, 0, tiled=True)  96 us
    all_to_all x3, waiting for transfers between devices, on_device(): across = lambda x, axis: lax.all_to_all(x, axis, 0, 0, tiled=True)  49.7 us
    all_to_all x3, starting transfers between devices, on_device(): across = lambda x, axis: lax.all_to_all(x, axis, 0, 0, tiled=True)  28.7 us
    pallas_call x1, Pallas kernels, on_device(): call(backward_forward, (chunks, kept), (flat, gathered))  6.09 us
    pallas_call x2, Pallas kernels, on_device(): call(back_call, (chunks, shape(static.shape, BF16)), (flat,))  4.63 us
  transfers between devices with their start and end apart: 3, of which 3 were waited for; matrix products, arithmetic and copies ran while one was open for 2% of the time, Pallas kernels for 1%

profile of v1, /device:TPU:2, one launch (start us, length us, event | category | flops | bytes accessed | tf_op | source)
XLA Modules:
  0.0 211.9 jit_solution(4873592136272830780)
XLA Ops:
  0.6 0.7 fusion.4
  1.6 0.7 fusion.pick_ref
  2.5 0.7 copy.18
  3.2 3.5 %forward_first.1 = (bf16[32,40,128]{2,1,0:T(8,128)(2,1)}, bf16[40,32,128]{2,1,0:T(8,128)(2,1)}) custom-call(bf16[2,5,4,4096]{3,2,1,0:T(4,128)(2,1)} %control_ref.1, bf16[256,64]{1,0:T(8,128)(2,1)} %fusion.pick_ref, bf16[1024,128]{1,0:T(8,128)(2,1)} %bitcast.32), custom_call_target="tpu_custom_call" | custom-call | tf_op jit(solution)/shard_map/forward_first/pallas_call | solution.py:250
  6.7 16.8 %all-to-all-start = ((bf16[32,40,128]{2,1,0:T(8,128)(2,1)}), bf16[32,40,128]{2,1,0:T(8,128)(2,1)S(1)}, u32[]{:S(2)}, u32[]{:S(2)}) async-start(bf16[32,40,128]{2,1,0:T(8,128)(2,1)} %get-tuple-element.12), calls=%async_computation | async-start | bytes 655360 | tf_op jit(solution)/shard_map/all_to_all | solution.py:248
  23.6 0.2 copy.19
  23.7 0.7 copy.20
  24.4 22.7 %all-to-all-done.recv_ref = bf16[32,40,128]{2,1,0:T(8,128)(2,1)S(1)} async-done(((bf16[32,40,128]{2,1,0:T(8,128)(2,1)}), bf16[32,40,128]{2,1,0:T(8,128)(2,1)S(1)}, u32[]{:S(2)}, u32[]{:S(2)}) %all-to-all-start) | async-done | bytes 327712 | tf_op jit(solution)/shard_map/all_to_all | solution.py:248
  47.1 0.7 copy-done.1
  47.8 2.1 ensemble.2
  49.9 6.1 %all-to-all-start.1 = ((bf16[16,40,128]{2,1,0:T(8,128)(2,1)}), bf16[16,40,128]{2,1,0:T(8,128)(2,1)S(1)}, u32[]{:S(2)}, u32[]{:S(2)}) async-start(bf16[16,40,128]{2,1,0:T(8,128)(2,1)} %ensemble.2), calls=%async_computation.1 | async-start | bytes 327680 | tf_op jit(solution)/shard_map/all_to_all | solution.py:248
  56.0 2.1 observations.1
  58.1 1.3 constant_dynamic-slice_fusion.root_ref
  59.4 5.2 %all-to-all-done.1.recv_ref = bf16[16,40,128]{2,1,0:T(8,128)(2,1)S(1)} async-done(((bf16[16,40,128]{2,1,0:T(8,128)(2,1)}), bf16[16,40,128]{2,1,0:T(8,128)(2,1)S(1)}, u32[]{:S(2)}, u32[]{:S(2)}) %all-to-all-start.1) | async-done | bytes 163872 | tf_op jit(solution)/shard_map/all_to_all | solution.py:248
  64.6 0.7 copy-done.2
  65.2 1.9 gradient.2
  67.1 12.7 %all_to_all.40.recv_ref = bf16[16,40,128]{2,1,0:T(8,128)(2,1)} all-to-all(bf16[16,40,128]{2,1,0:T(8,128)(2,1)} %gradient.2), channel_id=1, replica_groups=mesh['lev'=32,'mem'=16] {'mem'}, dimensions={0} | all-to-all | bytes 327680 | tf_op jit(solution)/shard_map/all_to_all | solution.py:248
  79.8 2.3 %backward.2 = (bf16[32,40,128]{2,1,0:T(8,128)(2,1)}, bf16[5,128,128]{2,1,0:T(8,128)(2,1)}) custom-call(bf16[16,40,128]{2,1,0:T(8,128)(2,1)} %all_to_all.40.recv_ref, bf16[2,5,128,128]{3,2,1,0:T(8,128)(2,1)} %perturb_ref.7, bf16[5,128,128]{2,1,0:T(8,128)(2,1)} %bitcast.27, bf16[5,128,128]{2,1,0:T(8,128)(2,1)} %root_ref.3, bf16[5,128,128]{2,1,0:T(8,128)(2,1)} %static_ref.3), custom_call_target="tpu_custom_call" | custom-call | tf_op jit(solution)/shard_map/backward/pallas_call | solution.py:259
  82.1 5.7 %all-to-all-start.3 = ((bf16[32,40,128]{2,1,0:T(8,128)(2,1)}), bf16[32,40,128]{2,1,0:T(8,128)(2,1)S(1)}, u32[]{:S(2)}, u32[]{:S(2)}) async-start(bf16[32,40,128]{2,1,0:T(8,128)(2,1)} %get-tuple-element.15), calls=%async_computation.3 | async-start | bytes 655360 | tf_op jit(solution)/shard_map/all_to_all | solution.py:248
  88.2 0.9 copy.22
  89.1 0.7 fusion.1.pick_t_ref
  89.8 21.8 %all-to-all-done.3.recv_ref = bf16[32,40,128]{2,1,0:T(8,128)(2,1)S(1)} async-done(((bf16[32,40,128]{2,1,0:T(8,128)(2,1)}), bf16[32,40,128]{2,1,0:T(8,128)(2,1)S(1)}, u32[]{:S(2)}, u32[]{:S(2)}) %all-to-all-start.3) | async-done | bytes 327712 | tf_op jit(solution)/shard_map/all_to_all | solution.py:248
  111.6 0.7 copy-done
  112.3 6.1 %backward_forward.1 = (bf16[32,40,128]{2,1,0:T(8,128)(2,1)}, bf16[40,32,128]{2,1,0:T(8,128)(2,1)}) custom-call(bf16[32,40,128]{2,1,0:T(8,128)(2,1)} %copy-done, bf16[40,32,128]{2,1,0:T(8,128)(2,1)} %get-tuple-element.16.kept_ref, bf16[256,64]{1,0:T(8,128)(2,1)} %fusion.1.pick_t_ref, bf16[1024,128]{1,0:T(8,128)(2,1)} %bitcast.30, ...), custom_call_target="tpu_custom_call" | custom-call | tf_op jit(solution)/shard_map/backward_forward/pallas_call | solution.py:264
  118.4 28.4 %all_to_all.41.recv_ref = bf16[32,40,128]{2,1,0:T(8,128)(2,1)} all-to-all(bf16[32,40,128]{2,1,0:T(8,128)(2,1)} %get-tuple-element.17), channel_id=1, replica_groups=mesh['lev'=32,'mem'=16] {'lev'}, dimensions={0} | all-to-all | bytes 655360 | tf_op jit(solution)/shard_map/all_to_all | solution.py:248
  146.8 2.1 ensemble.3
  148.9 12.7 %all_to_all.42.recv_ref = bf16[16,40,128]{2,1,0:T(8,128)(2,1)} all-to-all(bf16[16,40,128]{2,1,0:T(8,128)(2,1)} %ensemble.3), channel_id=1, replica_groups=mesh['lev'=32,'mem'=16] {'mem'}, dimensions={0} | all-to-all | bytes 327680 | tf_op jit(solution)/shard_map/all_to_all | solution.py:248
  161.6 1.9 gradient.3
  163.4 12.7 %all_to_all.43.recv_ref = bf16[16,40,128]{2,1,0:T(8,128)(2,1)} all-to-all(bf16[16,40,128]{2,1,0:T(8,128)(2,1)} %gradient.3), channel_id=1, replica_groups=mesh['lev'=32,'mem'=16] {'mem'}, dimensions={0} | all-to-all | bytes 327680 | tf_op jit(solution)/shard_map/all_to_all | solution.py:248
  176.1 2.3 %backward.3 = (bf16[32,40,128]{2,1,0:T(8,128)(2,1)}, bf16[5,128,128]{2,1,0:T(8,128)(2,1)}) custom-call(bf16[16,40,128]{2,1,0:T(8,128)(2,1)} %all_to_all.43.recv_ref, bf16[2,5,128,128]{3,2,1,0:T(8,128)(2,1)} %perturb_ref.7, bf16[5,128,128]{2,1,0:T(8,128)(2,1)} %bitcast.29, bf16[5,128,128]{2,1,0:T(8,128)(2,1)} %root_ref.3, ...), custom_call_target="tpu_custom_call" | custom-call | tf_op jit(solution)/shard_map/backward/pallas_call | solution.py:259
  178.4 29.6 %all_to_all.44.recv_ref = bf16[32,40,128]{2,1,0:T(8,128)(2,1)} all-to-all(bf16[32,40,128]{2,1,0:T(8,128)(2,1)} %get-tuple-element.19), channel_id=1, replica_groups=mesh['lev'=32,'mem'=16] {'lev'}, dimensions={0} | all-to-all | bytes 655360 | tf_op jit(solution)/shard_map/all_to_all | solution.py:248
  208.0 3.9 %backward_last.1 = bf16[2,5,4,4096]{3,2,1,0:T(4,128)(2,1)} custom-call(bf16[32,40,128]{2,1,0:T(8,128)(2,1)} %all_to_all.44.recv_ref, bf16[40,32,128]{2,1,0:T(8,128)(2,1)} %get-tuple-element.20.kept_ref, bf16[256,64]{1,0:T(8,128)(2,1)} %fusion.1.pick_t_ref, bf16[1024,128]{1,0:T(8,128)(2,1)} %bitcast.31), custom_call_target="tpu_custom_call" | custom-call | tf_op jit(solution)/shard_map/backward_last/pallas_call | solution.py:268
  (17 shorter events, 0.7 us)
Async XLA Ops:
  1.3 1.0 copy-start.3
  6.7 16.9 %copy-start.4 = (bf16[5,128,128]{2,1,0:T(8,128)(2,1)S(1)}, bf16[5,128,128]{2,1,0:T(8,128)(2,1)}, u32[]{:S(2)}) copy-start(bf16[5,128,128]{2,1,0:T(8,128)(2,1)} %param.16) | copy-start | bytes 491524
  6.7 40.4 %all-to-all-start = ((bf16[32,40,128]{2,1,0:T(8,128)(2,1)}), bf16[32,40,128]{2,1,0:T(8,128)(2,1)S(1)}, u32[]{:S(2)}, u32[]{:S(2)}) async-start(bf16[32,40,128]{2,1,0:T(8,128)(2,1)} %get-tuple-element.12), calls=%async_computation | async-start | bytes 655360 | tf_op jit(solution)/shard_map/all_to_all | solution.py:248
  47.1 0.7 copy-start.1
  49.9 14.7 %all-to-all-start.1 = ((bf16[16,40,128]{2,1,0:T(8,128)(2,1)}), bf16[16,40,128]{2,1,0:T(8,128)(2,1)S(1)}, u32[]{:S(2)}, u32[]{:S(2)}) async-start(bf16[16,40,128]{2,1,0:T(8,128)(2,1)} %ensemble.2), calls=%async_computation.1 | async-start | bytes 327680 | tf_op jit(solution)/shard_map/all_to_all | solution.py:248
  64.6 0.7 copy-start.2
  82.1 29.5 %all-to-all-start.3 = ((bf16[32,40,128]{2,1,0:T(8,128)(2,1)}), bf16[32,40,128]{2,1,0:T(8,128)(2,1)S(1)}, u32[]{:S(2)}, u32[]{:S(2)}) async-start(bf16[32,40,128]{2,1,0:T(8,128)(2,1)} %get-tuple-element.15), calls=%async_computation.3 | async-start | bytes 655360 | tf_op jit(solution)/shard_map/all_to_all | solution.py:248
  111.6 0.7 copy-start

commit v2 on v1

v2 whole, which is shorter than its diff:
```python
import functools
import math

import jax
import jax.numpy as jnp
from jax import lax
from jax.experimental import pallas as pl
from jax.experimental.pallas import tpu as pltpu
from jax.sharding import PartitionSpec as P

ITERS = 2

ENS_W = 0.85
STATIC_WEIGHT = 0.5
TAU = 0.5
HUBER_LOW = 0.3

F32 = jnp.float32
BF16 = jnp.bfloat16
LANES = 128
HALF = 64
SPANS = ((0, 5),)


def call(body, out_shape, scratch=(), *static):
    bound = functools.partial(body, *static)
    run = pl.pallas_call(bound, out_shape=out_shape, scratch_shapes=list(scratch), name=body.__name__)
    return lambda *args: run(*(pltpu.with_memory_space_constraint(a, pltpu.VMEM) for a in args))


def dot(a, b, dims=((1,), (0,))):
    return lax.dot_general(a, b, (dims, ((), ())), preferred_element_type=F32)


def spread(load, pick_ref, weight_ref, gathered):
    rows = gathered.shape[0] // 32
    lane = lax.broadcasted_iota(jnp.int32, (32, LANES), 1)
    pick = pick_ref[...]
    for first in range(0, rows, 2):
        columns = []
        for r in (first, first + 1):
            x = load(r)
            low = jnp.where(lane < HALF, x, 0.0)
            columns.append(jnp.concatenate([low, x - low], axis=0).astype(BF16))
        moved = dot(pick, jnp.concatenate(columns, axis=1)).astype(BF16)
        for i in range(2):
            for a in range(8):
                gathered[pl.ds((first + i) * 32, 32), pl.ds(a * LANES, LANES)] = moved[
                    a * 32 : a * 32 + 32, i * LANES : (i + 1) * LANES
                ]
    return dot(gathered[...], weight_ref[...])


def open_chunks(recv_ref, flat):
    rows = recv_ref.shape[1]
    for j in range(recv_ref.shape[0]):
        flat[pl.ds(j * rows, rows), :] = recv_ref[j].astype(F32)


def close_chunks(flat, send_ref):
    rows = send_ref.shape[1]
    for j in range(send_ref.shape[0]):
        send_ref[j] = flat[pl.ds(j * rows, rows), :].astype(BF16)


def by_row(flat, r, rows):
    return flat.at[pl.ds(r, 32, stride=rows), :]


def send_local(local, flat, send_ref):
    rows = send_ref.shape[1]
    for r in range(rows):
        by_row(flat, r, rows)[...] = local[r * 32 : r * 32 + 32]
    close_chunks(flat, send_ref)


def forward_first(span, control_ref, pick_ref, weight_ref, send_ref, kept_ref, flat, gathered):
    members, _, levels, columns = control_ref.shape
    rows = send_ref.shape[1]
    at = 0
    for m in range(members):
        for v in range(*span):
            x = control_ref[m, v].astype(F32)
            for j in range(columns // LANES):
                flat[pl.ds(j * rows + at, levels), :] = x[:, j * LANES : (j + 1) * LANES]
            at += levels

    def load(r):
        x = by_row(flat, r, rows)[...]
        kept_ref[r] = x.astype(BF16)
        return x

    send_local(spread(load, pick_ref, weight_ref, gathered), flat, send_ref)


def descend(recv_ref, kept_ref, pick_ref, weight_ref, flat, gathered):
    rows = recv_ref.shape[1]
    open_chunks(recv_ref, flat)
    adjoint = spread(lambda r: by_row(flat, r, rows)[...], pick_ref, weight_ref, gathered)
    current = kept_ref[...].astype(F32).reshape(rows * 32, LANES)
    return current - TAU * (current + adjoint)


def backward_forward(
    recv_ref, kept_ref, pick_t_ref, weight_t_ref, pick_ref, weight_ref, send_ref, next_ref, flat, gathered
):
    rows = recv_ref.shape[1]
    updated = descend(recv_ref, kept_ref, pick_t_ref, weight_t_ref, flat, gathered).astype(BF16)
    next_ref[...] = updated.reshape(rows, 32, LANES)
    local = spread(lambda r: next_ref[r].astype(F32), pick_ref, weight_ref, gathered)
    send_local(local, flat, send_ref)


def backward_last(spans, *refs):
    n = len(spans)
    recvs, helds = refs[:n], refs[n : 2 * n]
    pick_t_ref, weight_t_ref, control_ref = refs[2 * n : 2 * n + 3]
    scratch = refs[2 * n + 3 :]
    members, _, levels, columns = control_ref.shape
    for c, span in enumerate(spans):
        flat, gathered = scratch[2 * c], scratch[2 * c + 1]
        flat[...] = descend(recvs[c], helds[c], pick_t_ref, weight_t_ref, flat, gathered)
        start = 0
        for m in range(members):
            for v in range(*span):
                for j in range(columns // LANES):
                    x = flat[pl.ds(start + j, levels, stride=32), :]
                    control_ref[m, v, :, pl.ds(j * LANES, LANES)] = x.astype(BF16)
                start += levels * 32


def ensemble(span, recv_ref, perturb_ref, vert_ref, send_ref, flat):
    members = perturb_ref.shape[0]
    rows = recv_ref.shape[1]
    count = span[1] - span[0]
    levels = rows // (members * count)
    open_chunks(recv_ref, flat)
    totals = []
    for v in range(count):
        total = None
        for m in range(members):
            start = (m * count + v) * levels
            x = jnp.concatenate([by_row(flat, start + i, rows)[...] for i in range(levels)], axis=0)
            term = dot(vert_ref[span[0] + v], x.astype(BF16), ((0,), (0,)))
            term = term * perturb_ref[m, span[0] + v].astype(F32)
            total = term if total is None else total + term
        totals.append(total)
    deep = send_ref.shape[1] // count
    for d in range(send_ref.shape[0]):
        send_ref[d] = jnp.concatenate([t[d * deep : (d + 1) * deep] for t in totals], axis=0).astype(send_ref.dtype)


def observations(index_ref, value_ref, sigma_ref, mask_ref, slope_ref, shift_ref):
    cells = slope_ref.shape[0]
    weights = jnp.where(mask_ref[...] == 1, F32(1.0), F32(HUBER_LOW))
    precision = weights / (sigma_ref[...] * sigma_ref[...])
    pulled = precision * value_ref[...]
    index = index_ref[...]
    lefts, rights = [], []
    for o in range(index.shape[0]):
        at = index[o : o + 1]
        row = lax.broadcasted_iota(jnp.int32, (cells, LANES), 0) == at // LANES
        lane = lax.broadcasted_iota(jnp.int32, (LANES, LANES), 0) == at % LANES
        lefts.append(
            jnp.concatenate(
                [jnp.where(row, precision[o : o + 1], 0.0), jnp.where(row, pulled[o : o + 1], 0.0)], axis=0
            )
        )
        rights.append(jnp.where(lane, F32(1.0), F32(0.0)))
    both = lax.dot_general(
        jnp.concatenate(lefts, axis=1),
        jnp.concatenate(rights, axis=1),
        (((1,), (1,)), ((), ())),
        precision=lax.Precision.HIGHEST,
        preferred_element_type=F32,
    )
    slope_ref[...] = both[:cells]
    shift_ref[...] = both[cells:]


def gradient(gain, span, offset, recv_ref, static_ref, root_ref, slope_ref, shift_ref, send_ref):
    cells = recv_ref.shape[1]
    count = span[1] - span[0]
    deep = cells // count
    ens = jnp.sum(recv_ref[...].astype(F32), axis=0)
    static = jnp.concatenate([dot(root_ref[span[0] + v], static_ref[offset + v]) for v in range(count)], axis=0)
    increment = gain * ens + STATIC_WEIGHT * static
    own = pl.ds(span[0] * deep, cells)
    grad = (slope_ref[own, :] * increment - shift_ref[own, :]).astype(send_ref.dtype)
    for d in range(send_ref.shape[0]):
        send_ref[d] = grad


def backward(gain, span, offset, recv_ref, perturb_ref, vert_ref, root_ref, static_ref, send_ref, next_ref, flat):
    members, _, levels_all = perturb_ref.shape[:3]
    rows = send_ref.shape[1]
    count = span[1] - span[0]
    levels = rows // (members * count)
    deep = recv_ref.shape[1] // count
    field = recv_ref[...].astype(F32)
    for v in range(count):
        grad = field[:, v * deep : (v + 1) * deep, :].reshape(levels_all, LANES)
        for m in range(members):
            weighted = (gain * grad) * perturb_ref[m, span[0] + v].astype(F32)
            high = weighted.astype(BF16)
            low = (weighted - high.astype(F32)).astype(BF16)
            back = dot(vert_ref[span[0] + v], high) + dot(vert_ref[span[0] + v], low)
            start = (m * count + v) * levels
            for i in range(levels):
                by_row(flat, start + i, rows)[...] = back[i * 32 : i * 32 + 32]
        current = static_ref[offset + v].astype(F32)
        slope = current + STATIC_WEIGHT * dot(root_ref[span[0] + v], grad.astype(BF16), ((0,), (0,)))
        next_ref[v] = (current - TAU * slope).astype(BF16)
    close_chunks(flat, send_ref)


def tables(block_offset):
    count, slots = block_offset.shape
    blocks = jnp.arange(count, dtype=jnp.int32)
    source = (blocks[:, None] + block_offset) % count
    spot = (source % 2) * (count // 2) + source // 2
    by_slot = spot.reshape(count // 2, 2, slots).transpose(2, 1, 0)
    place = jnp.arange(count, dtype=jnp.int32)
    forth = by_slot.reshape(-1, 1) == place[None, :]
    back = (by_slot.reshape(slots, 1, count) == place[None, :, None]).reshape(slots * count, count)
    return forth.astype(BF16), back.astype(BF16)


def weights(tiles):
    slots, width = tiles.shape[:2]
    left = jnp.pad(tiles, ((0, 0), (0, 0), (0, width)))
    right = jnp.pad(tiles, ((0, 0), (0, 0), (width, 0)))
    both = jnp.stack([left, left, right, right], axis=1)
    return both.reshape(slots * 4 * width, 2 * width)


def on_device(
    control,
    static_control_vector,
    perturb,
    tiles,
    block_offset,
    vert,
    static_vertical_root,
    obs_index,
    obs_value,
    obs_sigma,
    huber_mask,
):
    n_lev, n_mem = lax.axis_size("lev"), lax.axis_size("mem")
    members, variables, levels, columns = control.shape
    levels_all = vert.shape[1]
    deep = levels_all // n_mem
    gain = ENS_W / math.sqrt(members * n_mem)

    pick, pick_t = tables(block_offset)
    weight, weight_t = weights(tiles), weights(jnp.swapaxes(tiles, 1, 2))
    turned = vert.reshape(variables, levels_all, n_lev, levels).transpose(0, 3, 2, 1).reshape(vert.shape)
    own_root = lax.dynamic_slice_in_dim(static_vertical_root, lax.axis_index("mem") * deep, deep, 1)

    shape = pltpu.VMEM
    field = shape((variables * deep, LANES), F32)
    flat_obs = lambda x: x.reshape(-1, LANES)
    across = lambda x, axis: lax.all_to_all(x, axis, 0, 0, tiled=True)

    rows = [members * (b - a) * levels for a, b in SPANS]
    chunks = [shape((n_lev, r, LANES), BF16) for r in rows]
    kept = [shape((r, n_lev, LANES), BF16) for r in rows]
    parts = [shape((n_mem, (b - a) * deep, LANES), BF16) for a, b in SPANS]
    statics = [shape((b - a, *static_control_vector.shape[1:]), BF16) for a, b in SPANS]
    flat = [pltpu.VMEM((n_lev * r, LANES), F32) for r in rows]
    both = [(f, pltpu.VMEM((n_lev * r, 8 * LANES), BF16)) for f, r in zip(flat, rows)]
    every = range(len(SPANS))

    send, held = [None] * len(SPANS), [None] * len(SPANS)
    static = [static_control_vector] * len(SPANS)
    offset = [a for a, _ in SPANS]
    for c in every:
        send[c], held[c] = call(forward_first, (chunks[c], kept[c]), both[c], SPANS[c])(control, pick, weight)
        send[c] = across(send[c], "lev")
    slope, shift = call(observations, (field, field))(
        flat_obs(obs_index), flat_obs(obs_value), flat_obs(obs_sigma), flat_obs(huber_mask)
    )
    for turn in range(ITERS):
        for c in every:
            send[c] = call(ensemble, parts[c], flat[c : c + 1], SPANS[c])(send[c], perturb, turned)
            send[c] = across(send[c], "mem")
        for c in every:
            send[c] = call(gradient, parts[c], (), gain, SPANS[c], offset[c])(
                send[c], static[c], own_root, slope, shift
            )
            send[c] = across(send[c], "mem")
        for c in every:
            send[c], static[c] = call(backward, (chunks[c], statics[c]), flat[c : c + 1], gain, SPANS[c], offset[c])(
                send[c], perturb, turned, static_vertical_root, static[c]
            )
            offset[c] = 0
            send[c] = across(send[c], "lev")
        for c in every:
            if turn + 1 < ITERS:
                send[c], held[c] = call(backward_forward, (chunks[c], kept[c]), both[c])(
                    send[c], held[c], pick_t, weight_t, pick, weight
                )
                send[c] = across(send[c], "lev")
    scratch = [buffer for pair in both for buffer in pair]
    control = call(backward_last, shape(control.shape, BF16), scratch, SPANS)(*send, *held, pick_t, weight_t)
    return (control, jnp.concatenate(static, axis=0))


def solution(mesh):
    placed = (
        P("mem", None, "lev", None),
        P(None, None, "lev"),
        P("mem", None, None, "lev"),
        P(),
        P(),
        P(),
        P(),
        P(("lev", "mem")),
        P(("lev", "mem")),
        P(("lev", "mem")),
        P(("lev", "mem")),
    )
    return jax.shard_map(
        on_device,
        mesh=mesh,
        in_specs=placed,
        out_specs=(P("mem", None, "lev", None), P(None, None, "lev")),
        check_vma=False,
    )
```

time: 213 us -> 193 us (0.906)
  blocking collectives: 96 us -> 61.4 us
  waiting for transfers between devices: 49.7 us -> 76.5 us
  Pallas kernels: 28 us -> 13 us
  starting transfers between devices: 28.7 us -> 34 us
    all_to_all x5 -> x4, blocking collectives: 96 us -> 61.4 us  [on_device(): across = lambda x, axis: lax.all_to_all(x, axis, 0, 0, tiled=True)]
    all_to_all x3 -> x4, waiting for transfers between devices: 49.7 us -> 76.5 us  [on_device(): across = lambda x, axis: lax.all_to_all(x, axis, 0, 0, tiled=True)]
    pallas_call x10, Pallas kernels: 28 us -> 13 us  [call(): run(*(pltpu.with_memory_space_constraint(a, pltpu.VMEM) for a in args))]
    all_to_all x3 -> x4, starting transfers between devices: 28.7 us -> 34 us  [on_device(): across = lambda x, axis: lax.all_to_all(x, axis, 0, 0, tiled=True)]
    unnamed x11 -> x35, local copies, waits for them, and re-layouts: 2.29 us -> 5.07 us
  transfers between devices with their start and end apart: 3 -> 4, of which waited for: 3 -> 4; matrix products, arithmetic and copies ran while one was open for 2% -> 1% of each run, Pallas kernels for 1% -> 0%
where the time goes in v2:
time: 193 us
  waiting for transfers between devices  76.5 us (40%)
  blocking collectives  61.4 us (32%)
  starting transfers between devices  34 us (18%)
  Pallas kernels  13 us (7%)
  local copies, waits for them, and re-layouts  5.93 us (3%)
    all_to_all x4, waiting for transfers between devices, on_device(): across = lambda x, axis: lax.all_to_all(x, axis, 0, 0, tiled=True)  76.5 us
    all_to_all x4, blocking collectives, on_device(): across = lambda x, axis: lax.all_to_all(x, axis, 0, 0, tiled=True)  61.4 us
    all_to_all x4, starting transfers between devices, on_device(): across = lambda x, axis: lax.all_to_all(x, axis, 0, 0, tiled=True)  34 us
    pallas_call x10, Pallas kernels, call(): run(*(pltpu.with_memory_space_constraint(a, pltpu.VMEM) for a in args))  13 us
    unnamed x35, local copies, waits for them, and re-layouts  5.07 us
  transfers between devices with their start and end apart: 4, of which 4 were waited for; matrix products, arithmetic and copies ran while one was open for 1% of the time, Pallas kernels for 0%

profile of v2, /device:TPU:2, one launch (start us, length us, event | category | flops | bytes accessed | tf_op | source)
XLA Modules:
  0.0 192.6 jit_solution(13869632574682812180)
XLA Ops:
  0.6 0.7 fusion.4
  1.7 0.4 copy-done.14
  2.3 0.9 copy-done.9
  3.3 2.4 %forward_first.1 = (bf16[32,40,128]{2,1,0:T(8,128)(2,1)}, bf16[40,32,128]{2,1,0:T(8,128)(2,1)S(1)}) custom-call(bf16[2,5,4,4096]{3,2,1,0:T(4,128)(2,1)S(1)} %copy-done.9, bf16[256,64]{1,0:T(8,128)(2,1)S(1)} %fusion.pick_ref, bf16[1024,128]{1,0:T(8,128)(2,1)S(1)} %bitcast.32), custom_call_target="tpu_custom_call" | custom-call | tf_op jit(solution)/shard_map/forward_first/pallas_call | solution.py:28
  5.7 0.7 copy-done.5
  6.4 16.8 %all-to-all-start = ((bf16[32,40,128]{2,1,0:T(8,128)(2,1)}), bf16[32,40,128]{2,1,0:T(8,128)(2,1)S(1)}, u32[]{:S(2)}, u32[]{:S(2)}) async-start(bf16[32,40,128]{2,1,0:T(8,128)(2,1)} %get-tuple-element.12), calls=%async_computation | async-start | bytes 655360 | tf_op jit(solution)/shard_map/all_to_all | solution.py:264
  23.3 0.2 copy.19
  23.5 23.3 %all-to-all-done.recv_ref = bf16[32,40,128]{2,1,0:T(8,128)(2,1)S(1)} async-done(((bf16[32,40,128]{2,1,0:T(8,128)(2,1)}), bf16[32,40,128]{2,1,0:T(8,128)(2,1)S(1)}, u32[]{:S(2)}, u32[]{:S(2)}) %all-to-all-start) | async-done | bytes 327712 | tf_op jit(solution)/shard_map/all_to_all | solution.py:264
  46.8 1.0 ensemble.2
  47.8 6.3 %all-to-all-start.1 = ((bf16[16,40,128]{2,1,0:T(8,128)(2,1)}), bf16[16,40,128]{2,1,0:T(8,128)(2,1)S(1)}, u32[]{:S(2)}, u32[]{:S(2)}) async-start(bf16[16,40,128]{2,1,0:T(8,128)(2,1)} %ensemble.2), calls=%async_computation.1 | async-start | bytes 327680 | tf_op jit(solution)/shard_map/all_to_all | solution.py:264
  54.1 0.6 copy-done.12
  54.8 0.7 observations.1
  55.5 7.1 %all-to-all-done.1.recv_ref = bf16[16,40,128]{2,1,0:T(8,128)(2,1)S(1)} async-done(((bf16[16,40,128]{2,1,0:T(8,128)(2,1)}), bf16[16,40,128]{2,1,0:T(8,128)(2,1)S(1)}, u32[]{:S(2)}, u32[]{:S(2)}) %all-to-all-start.1) | async-done | bytes 163872 | tf_op jit(solution)/shard_map/all_to_all | solution.py:264
  62.6 0.2 gradient.2
  62.8 11.1 %all_to_all.40.recv_ref = bf16[16,40,128]{2,1,0:T(8,128)(2,1)S(1)} all-to-all(bf16[16,40,128]{2,1,0:T(8,128)(2,1)S(1)} %gradient.2), channel_id=1, replica_groups=mesh['lev'=32,'mem'=16] {'mem'}, dimensions={0} | all-to-all | bytes 327680 | tf_op jit(solution)/shard_map/all_to_all | solution.py:264
  73.9 1.1 backward.2
  75.0 0.7 copy-done.3
  75.7 5.7 %all-to-all-start.3 = ((bf16[32,40,128]{2,1,0:T(8,128)(2,1)}), bf16[32,40,128]{2,1,0:T(8,128)(2,1)S(1)}, u32[]{:S(2)}, u32[]{:S(2)}) async-start(bf16[32,40,128]{2,1,0:T(8,128)(2,1)} %get-tuple-element.15), calls=%async_computation.3 | async-start | bytes 655360 | tf_op jit(solution)/shard_map/all_to_all | solution.py:264
  81.8 0.2 copy.22
  82.1 23.1 %all-to-all-done.3.recv_ref = bf16[32,40,128]{2,1,0:T(8,128)(2,1)S(1)} async-done(((bf16[32,40,128]{2,1,0:T(8,128)(2,1)}), bf16[32,40,128]{2,1,0:T(8,128)(2,1)S(1)}, u32[]{:S(2)}, u32[]{:S(2)}) %all-to-all-start.3) | async-done | bytes 327712 | tf_op jit(solution)/shard_map/all_to_all | solution.py:264
  105.2 4.1 %backward_forward.1 = (bf16[32,40,128]{2,1,0:T(8,128)(2,1)S(1)}, bf16[40,32,128]{2,1,0:T(8,128)(2,1)S(1)}) custom-call(bf16[32,40,128]{2,1,0:T(8,128)(2,1)S(1)} %all-to-all-done.3.recv_ref, bf16[40,32,128]{2,1,0:T(8,128)(2,1)S(1)} %copy-done.6, bf16[256,64]{1,0:T(8,128)(2,1)S(1)} %fusion.1.pick_t_ref.refs_2_, bf16[1024,128]{1,0:T(8,128)(2,1)S(1)} %bitcast.30, ...), custom_call_target="tpu_custom_call" | custom-call | tf_op jit(solution)/shard_map/backward_forward/pallas_call | solution.py:28
  109.3 27.8 %all_to_all.41.recv_ref = bf16[32,40,128]{2,1,0:T(8,128)(2,1)S(1)} all-to-all(bf16[32,40,128]{2,1,0:T(8,128)(2,1)S(1)} %get-tuple-element.17), channel_id=1, replica_groups=mesh['lev'=32,'mem'=16] {'lev'}, dimensions={0} | all-to-all | bytes 655360 | tf_op jit(solution)/shard_map/all_to_all | solution.py:264
  137.2 0.3 ensemble.3
  137.5 11.3 %all_to_all.42.recv_ref = bf16[16,40,128]{2,1,0:T(8,128)(2,1)S(1)} all-to-all(bf16[16,40,128]{2,1,0:T(8,128)(2,1)S(1)} %ensemble.3), channel_id=1, replica_groups=mesh['lev'=32,'mem'=16] {'mem'}, dimensions={0} | all-to-all | bytes 327680 | tf_op jit(solution)/shard_map/all_to_all | solution.py:264
  148.7 0.2 gradient.3
  148.9 11.1 %all_to_all.43.recv_ref = bf16[16,40,128]{2,1,0:T(8,128)(2,1)S(1)} all-to-all(bf16[16,40,128]{2,1,0:T(8,128)(2,1)S(1)} %gradient.3), channel_id=1, replica_groups=mesh['lev'=32,'mem'=16] {'mem'}, dimensions={0} | all-to-all | bytes 327680 | tf_op jit(solution)/shard_map/all_to_all | solution.py:264
  160.0 1.1 backward.3
  161.2 5.1 %all-to-all-start.7 = ((bf16[32,40,128]{2,1,0:T(8,128)(2,1)}), bf16[32,40,128]{2,1,0:T(8,128)(2,1)S(1)}, u32[]{:S(2)}, u32[]{:S(2)}) async-start(bf16[32,40,128]{2,1,0:T(8,128)(2,1)} %get-tuple-element.19), calls=%async_computation.7 | async-start | bytes 655360 | tf_op jit(solution)/shard_map/all_to_all | solution.py:264
  166.3 0.7 copy.24
  167.0 23.1 %all-to-all-done.7.refs_0_ = bf16[32,40,128]{2,1,0:T(8,128)(2,1)S(1)} async-done(((bf16[32,40,128]{2,1,0:T(8,128)(2,1)}), bf16[32,40,128]{2,1,0:T(8,128)(2,1)S(1)}, u32[]{:S(2)}, u32[]{:S(2)}) %all-to-all-start.7) | async-done | bytes 327712 | tf_op jit(solution)/shard_map/all_to_all | solution.py:264
  190.0 1.9 backward_last.1
  191.9 0.7 copy.23
  (42 shorter events, 1.0 us)
Async XLA Ops:
  1.3 0.8 copy-start.14
  2.3 1.0 copy-start.9
  5.7 0.7 copy-start.5
  6.4 16.9 %copy-start.15 = (bf16[5,128,128]{2,1,0:T(8,128)(2,1)S(1)}, bf16[5,128,128]{2,1,0:T(8,128)(2,1)}, u32[]{:S(2)}) copy-start(bf16[5,128,128]{2,1,0:T(8,128)(2,1)} %param.16) | copy-start | bytes 491524
  6.4 40.4 %all-to-all-start = ((bf16[32,40,128]{2,1,0:T(8,128)(2,1)}), bf16[32,40,128]{2,1,0:T(8,128)(2,1)S(1)}, u32[]{:S(2)}, u32[]{:S(2)}) async-start(bf16[32,40,128]{2,1,0:T(8,128)(2,1)} %get-tuple-element.12), calls=%async_computation | async-start | bytes 655360 | tf_op jit(solution)/shard_map/all_to_all | solution.py:264
  23.3 23.5 %copy-start = (bf16[2,5,128,128]{3,2,1,0:T(8,128)(2,1)S(1)}, bf16[2,5,128,128]{3,2,1,0:T(8,128)(2,1)}, u32[]{:S(2)}) copy-start(bf16[2,5,128,128]{3,2,1,0:T(8,128)(2,1)} %perturb_ref.7) | copy-start | bytes 983044
  47.8 6.3 %copy-start.13 = (s32[1024]{0:T(1024)S(1)}, s32[1024]{0:T(1024)}, u32[]{:S(2)}) copy-start(s32[1024]{0:T(1024)} %param.21) | copy-start | bytes 12292
  47.8 7.7 %copy-start.1 = (bf16[5,128,128]{2,1,0:T(8,128)(2,1)S(1)}, bf16[5,128,128]{2,1,0:T(8,128)(2,1)}, u32[]{:S(2)}) copy-start(bf16[5,128,128]{2,1,0:T(8,128)(2,1)} %root_ref.3) | copy-start | bytes 491524
  47.8 14.8 %copy-start.2 = (bf16[5,128,128]{2,1,0:T(8,128)(2,1)S(1)}, bf16[5,128,128]{2,1,0:T(8,128)(2,1)}, u32[]{:S(2)}) copy-start(bf16[5,128,128]{2,1,0:T(8,128)(2,1)} %static_ref.3) | copy-start | bytes 491524
  47.8 14.8 %all-to-all-start.1 = ((bf16[16,40,128]{2,1,0:T(8,128)(2,1)}), bf16[16,40,128]{2,1,0:T(8,128)(2,1)S(1)}, u32[]{:S(2)}, u32[]{:S(2)}) async-start(bf16[16,40,128]{2,1,0:T(8,128)(2,1)} %ensemble.2), calls=%async_computation.1 | async-start | bytes 327680 | tf_op jit(solution)/shard_map/all_to_all | solution.py:264
  54.1 0.7 copy-start.12
  54.1 0.7 copy-start.11
  54.1 0.7 copy-start.10
  75.0 0.7 copy-start.3
  75.7 29.5 %all-to-all-start.3 = ((bf16[32,40,128]{2,1,0:T(8,128)(2,1)}), bf16[32,40,128]{2,1,0:T(8,128)(2,1)S(1)}, u32[]{:S(2)}, u32[]{:S(2)}) async-start(bf16[32,40,128]{2,1,0:T(8,128)(2,1)} %get-tuple-element.15), calls=%async_computation.3 | async-start | bytes 655360 | tf_op jit(solution)/shard_map/all_to_all | solution.py:264
  81.7 23.4 %copy-start.6 = (bf16[40,32,128]{2,1,0:T(8,128)(2,1)S(1)}, bf16[40,32,128]{2,1,0:T(8,128)(2,1)}, u32[]{:S(2)}) copy-start(bf16[40,32,128]{2,1,0:T(8,128)(2,1)} %copy-done.5) | copy-start | bytes 983044
  109.3 27.9 %copy-start.7 = (bf16[40,32,128]{2,1,0:T(8,128)(2,1)}, bf16[40,32,128]{2,1,0:T(8,128)(2,1)S(1)}, u32[]{:S(2)}) copy-start(bf16[40,32,128]{2,1,0:T(8,128)(2,1)S(1)} %get-tuple-element.20.refs_1_) | copy-start | bytes 983044
  137.5 11.3 %copy-start.4 = (bf16[5,128,128]{2,1,0:T(8,128)(2,1)S(1)}, bf16[5,128,128]{2,1,0:T(8,128)(2,1)}, u32[]{:S(2)}) copy-start(bf16[5,128,128]{2,1,0:T(8,128)(2,1)} %copy-done.3) | copy-start | bytes 491524
  161.2 28.9 %all-to-all-start.7 = ((bf16[32,40,128]{2,1,0:T(8,128)(2,1)}), bf16[32,40,128]{2,1,0:T(8,128)(2,1)S(1)}, u32[]{:S(2)}, u32[]{:S(2)}) async-start(bf16[32,40,128]{2,1,0:T(8,128)(2,1)} %get-tuple-element.19), calls=%async_computation.7 | async-start | bytes 655360 | tf_op jit(solution)/shard_map/all_to_all | solution.py:264
  166.3 23.7 %copy-start.8 = (bf16[40,32,128]{2,1,0:T(8,128)(2,1)S(1)}, bf16[40,32,128]{2,1,0:T(8,128)(2,1)}, u32[]{:S(2)}) copy-start(bf16[40,32,128]{2,1,0:T(8,128)(2,1)} %copy-done.7) | copy-start | bytes 983044

commit v3 on v1

v3 whole, which is shorter than its diff:
```python
import functools
import math

import jax
import jax.numpy as jnp
from jax import lax
from jax.experimental import pallas as pl
from jax.experimental.pallas import tpu as pltpu
from jax.sharding import PartitionSpec as P

ITERS = 2

ENS_W = 0.85
STATIC_WEIGHT = 0.5
TAU = 0.5
HUBER_LOW = 0.3

F32 = jnp.float32
BF16 = jnp.bfloat16
LANES = 128
HALF = 64
PAIRS = 32
BLOCKS = 64
GROUP = 5


def call(body, out_shape, scratch, args, stay=(), **static):
    run = pl.pallas_call(
        functools.partial(body, **static),
        out_shape=out_shape,
        in_specs=[pl.BlockSpec(memory_space=pl.ANY if i in stay else pltpu.VMEM) for i in range(len(args))],
        scratch_shapes=list(scratch),
        name=body.__name__,
    )
    return run(*(a if i in stay else pltpu.with_memory_space_constraint(a, pltpu.VMEM) for i, a in enumerate(args)))


def dot(a, b, dims=((1,), (0,))):
    return lax.dot_general(a, b, (dims, ((), ())), preferred_element_type=F32)


def iota(shape, axis):
    return lax.broadcasted_iota(jnp.int32, shape, axis)


def ones(mask):
    return jnp.where(mask, F32(1.0), F32(0.0)).astype(BF16)


def swap_halves(x, y):
    low = iota(x.shape, 1) < HALF
    first = jnp.where(low, x, pltpu.roll(y, HALF, 1))
    second = jnp.where(low, pltpu.roll(x, HALF, 1), y)
    return first, second


def spread(load, store, pick_ref, weight_ref, moved_ref):
    count = moved_ref.shape[0] // BLOCKS
    pick = pick_ref[...]
    for g in range(0, count, GROUP):
        group = [jnp.concatenate(swap_halves(load(2 * p), load(2 * p + 1)), axis=0) for p in range(g, g + GROUP)]
        moved = dot(pick, jnp.concatenate(group, axis=1).astype(BF16)).astype(BF16)
        for i in range(GROUP):
            for k in range(pick.shape[0] // BLOCKS):
                moved_ref[pl.ds((g + i) * BLOCKS, BLOCKS), pl.ds(k * LANES, LANES)] = moved[
                    k * BLOCKS : (k + 1) * BLOCKS, i * LANES : (i + 1) * LANES
                ]
        out = dot(moved_ref[pl.ds(g * BLOCKS, GROUP * BLOCKS), :], weight_ref[...])
        for p in range(GROUP):
            at = p * BLOCKS
            x, y = swap_halves(out[at : at + PAIRS], out[at + PAIRS : at + BLOCKS])
            store(2 * (g + p), x)
            store(2 * (g + p) + 1, y)


def open_chunks(recv_ref, flat):
    rows = recv_ref.shape[1]
    for j in range(recv_ref.shape[0]):
        flat[pl.ds(j * rows, rows), :] = recv_ref[j].astype(F32)


def close_chunks(flat, send_ref):
    rows = send_ref.shape[1]
    for j in range(send_ref.shape[0]):
        send_ref[j] = flat[pl.ds(j * rows, rows), :].astype(BF16)


def by_row(flat, rows):
    at = lambda r: pl.ds(r, PAIRS, stride=rows)

    def load(r):
        return flat[at(r), :]

    def store(r, x):
        flat[at(r), :] = x

    return load, store


def forward_first(
    control_hbm,
    offset_hbm,
    tiles_hbm,
    send_ref,
    kept_hbm,
    flat,
    moved,
    pick,
    weight,
    kept,
    control,
    offset_ref,
    tiles_ref,
    sems,
):
    members, variables, levels, columns = control.shape
    rows = send_ref.shape[1]
    fetch = [pltpu.make_async_copy(control_hbm.at[m], control.at[m], sems.at[m]) for m in range(members)]
    small = [
        pltpu.make_async_copy(offset_hbm, offset_ref, sems.at[members + 1]),
        pltpu.make_async_copy(tiles_hbm, tiles_ref, sems.at[members + 2]),
    ]
    for copy in small + fetch:
        copy.start()
    for copy in small:
        copy.wait()
    square = (BLOCKS, BLOCKS)
    block = iota(square, 1)
    turn = ones(iota(square, 0) == (block & 1) * PAIRS + (block >> 1))
    wide = (HALF, LANES)
    left, right = ones(iota(wide, 1) == iota(wide, 0)), ones(iota(wide, 1) == iota(wide, 0) + HALF)
    for k in range(tiles_ref.shape[0]):
        source = (block[:1] + offset_ref[k : k + 1, :]) & (BLOCKS - 1)
        spot = (source & 1) * PAIRS + (source >> 1)
        found = ones(iota(square, 0) == spot)
        pick[pl.ds(k * BLOCKS, BLOCKS), :] = dot(turn, found, ((1,), (1,))).astype(BF16)
        tile = tiles_ref[k]
        weight[pl.ds(2 * k * HALF, HALF), :] = dot(tile, left).astype(BF16)
        weight[pl.ds((2 * k + 1) * HALF, HALF), :] = dot(tile, right).astype(BF16)
    for m in range(members):
        fetch[m].wait()
        for v in range(variables):
            x = control[m, v].astype(F32)
            at = (m * variables + v) * levels
            for j in range(columns // LANES):
                flat[pl.ds(j * rows + at, levels), :] = x[:, j * LANES : (j + 1) * LANES]

    load, store = by_row(flat, rows)

    def load_kept(r):
        x = load(r)
        kept[r] = x.astype(BF16)
        return x

    keep = pltpu.make_async_copy(kept, kept_hbm, sems.at[members])
    spread(load_kept, store, pick, weight, moved)
    keep.start()
    close_chunks(flat, send_ref)
    keep.wait()


def by_variable(recv_ref, variables):
    deep = recv_ref.shape[1] // variables
    field = recv_ref[...].astype(F32)
    return [field[:, v * deep : (v + 1) * deep, :].reshape(-1, LANES) for v in range(variables)]


def descend_static(grad_ref, root_ref, static_ref, next_ref):
    for v, grad in enumerate(by_variable(grad_ref, static_ref.shape[0])):
        current = static_ref[v].astype(F32)
        slope = current + STATIC_WEIGHT * dot(root_ref[v], grad.astype(BF16))
        next_ref[v] = (current - TAU * slope).astype(BF16)


def backward_forward(
    recv_ref,
    kept_ref,
    pick_t_ref,
    weight_t_ref,
    grad_ref,
    root_ref,
    static_ref,
    pick_ref,
    weight_ref,
    send_ref,
    next_hbm,
    moving_hbm,
    flat,
    moved,
    next_ref,
    moving_ref,
    sems,
):
    descend_static(grad_ref, root_ref, static_ref, moving_ref)
    keep_static = pltpu.make_async_copy(moving_ref, moving_hbm, sems.at[0])
    keep_static.start()
    load, store = by_row(flat, recv_ref.shape[1])
    open_chunks(recv_ref, flat)

    def update(r, adjoint):
        current = kept_ref[r].astype(F32)
        next_ref[r] = (current - TAU * (current + adjoint)).astype(BF16)

    keep = pltpu.make_async_copy(next_ref, next_hbm, sems.at[1])
    spread(load, update, pick_t_ref, weight_t_ref, moved)
    keep.start()
    spread(lambda r: next_ref[r].astype(F32), store, pick_ref, weight_ref, moved)
    close_chunks(flat, send_ref)
    keep_static.wait()
    keep.wait()


def backward_last(
    recv_ref,
    kept_ref,
    pick_t_ref,
    weight_t_ref,
    grad_ref,
    root_ref,
    static_ref,
    control_hbm,
    moving_hbm,
    flat,
    moved,
    final,
    control,
    moving_ref,
    sems,
):
    members, variables, levels, columns = control.shape
    descend_static(grad_ref, root_ref, static_ref, moving_ref)
    keep_static = pltpu.make_async_copy(moving_ref, moving_hbm, sems.at[members])
    keep_static.start()
    load, _ = by_row(flat, recv_ref.shape[1])
    open_chunks(recv_ref, flat)

    def update(r, adjoint):
        current = kept_ref[r].astype(F32)
        final[pl.ds(r * PAIRS, PAIRS), :] = current - TAU * (current + adjoint)

    spread(load, update, pick_t_ref, weight_t_ref, moved)
    copies = [pltpu.make_async_copy(control.at[m], control_hbm.at[m], sems.at[m]) for m in range(members)]
    for m in range(members):
        for v in range(variables):
            start = (m * variables + v) * levels * PAIRS
            for j in range(columns // LANES):
                x = final[pl.ds(start + j, levels, stride=PAIRS), :]
                control[m, v, :, pl.ds(j * LANES, LANES)] = x.astype(BF16)
        copies[m].start()
    keep_static.wait()
    for copy in copies:
        copy.wait()


def ensemble(recv_ref, perturb_ref, vert_ref, send_ref, flat):
    members, variables = perturb_ref.shape[:2]
    rows = recv_ref.shape[1]
    levels = rows // (members * variables)
    load, _ = by_row(flat, rows)
    open_chunks(recv_ref, flat)
    totals = []
    for v in range(variables):
        total = None
        for m in range(members):
            start = (m * variables + v) * levels
            x = jnp.concatenate([load(start + i) for i in range(levels)], axis=0).astype(BF16)
            term = dot(vert_ref[v], x, ((0,), (0,))) * perturb_ref[m, v].astype(F32)
            total = term if total is None else total + term
        totals.append(total)
    deep = send_ref.shape[1] // variables
    for d in range(send_ref.shape[0]):
        send_ref[d] = jnp.concatenate([t[d * deep : (d + 1) * deep] for t in totals], axis=0).astype(send_ref.dtype)


def observations(index_ref, value_ref, sigma_ref, mask_ref, slope_ref, shift_ref):
    cells = slope_ref.shape[0]
    weights = jnp.where(mask_ref[...] == 1, F32(1.0), F32(HUBER_LOW))
    precision = weights / (sigma_ref[...] * sigma_ref[...])
    pulled = precision * value_ref[...]
    index = index_ref[...]
    lefts, rights = [], []
    for o in range(index.shape[0]):
        at = index[o : o + 1]
        row = iota((cells, LANES), 0) == at // LANES
        lane = iota((LANES, LANES), 0) == at % LANES
        lefts.append(
            jnp.concatenate(
                [jnp.where(row, precision[o : o + 1], 0.0), jnp.where(row, pulled[o : o + 1], 0.0)], axis=0
            )
        )
        rights.append(jnp.where(lane, F32(1.0), F32(0.0)))
    both = lax.dot_general(
        jnp.concatenate(lefts, axis=1),
        jnp.concatenate(rights, axis=1),
        (((1,), (1,)), ((), ())),
        precision=lax.Precision.HIGHEST,
        preferred_element_type=F32,
    )
    slope_ref[...] = both[:cells]
    shift_ref[...] = both[cells:]


def gradient(recv_ref, static_ref, root_ref, slope_ref, shift_ref, send_ref, *, gain):
    ens = jnp.sum(recv_ref[...].astype(F32), axis=0)
    static = jnp.concatenate([dot(root_ref[v], static_ref[v]) for v in range(static_ref.shape[0])], axis=0)
    increment = gain * ens + STATIC_WEIGHT * static
    grad = (slope_ref[...] * increment - shift_ref[...]).astype(send_ref.dtype)
    for d in range(send_ref.shape[0]):
        send_ref[d] = grad


def backward(recv_ref, perturb_ref, vert_ref, send_ref, flat, *, gain):
    members, variables = perturb_ref.shape[:2]
    rows = send_ref.shape[1]
    levels = rows // (members * variables)
    _, store = by_row(flat, rows)
    grads = by_variable(recv_ref, variables)
    for v in range(variables):
        for m in range(members):
            weighted = (gain * grads[v]) * perturb_ref[m, v].astype(F32)
            high = weighted.astype(BF16)
            low = (weighted - high.astype(F32)).astype(BF16)
            back = dot(vert_ref[v], high) + dot(vert_ref[v], low)
            start = (m * variables + v) * levels
            for i in range(levels):
                store(start + i, back[i * PAIRS : (i + 1) * PAIRS])
    close_chunks(flat, send_ref)


def tables(block_offset):
    count, slots = block_offset.shape
    blocks = jnp.arange(count, dtype=jnp.int32)
    source = (blocks[:, None] + block_offset) % count
    spot = (source % 2) * (count // 2) + source // 2
    by_slot = spot.reshape(count // 2, 2, slots).transpose(2, 1, 0)
    forth = by_slot.reshape(-1, 1) == blocks[None, :]
    back = (by_slot.reshape(slots, 1, count) == blocks[None, :, None]).reshape(slots * count, count)
    return forth.astype(BF16), back.astype(BF16)


def weights(tiles):
    slots, width = tiles.shape[:2]
    left = jnp.pad(tiles, ((0, 0), (0, 0), (0, width)))
    right = jnp.pad(tiles, ((0, 0), (0, 0), (width, 0)))
    return jnp.stack([left, right], axis=1).reshape(slots * 2 * width, 2 * width)


def on_device(
    control,
    static_control_vector,
    perturb,
    tiles,
    block_offset,
    vert,
    static_vertical_root,
    obs_index,
    obs_value,
    obs_sigma,
    huber_mask,
):
    n_lev, n_mem = lax.axis_size("lev"), lax.axis_size("mem")
    members, variables, levels, columns = control.shape
    levels_all = vert.shape[1]
    deep = levels_all // n_mem
    rows = members * variables * levels
    slots = tiles.shape[0]
    gain = ENS_W / math.sqrt(members * n_mem)

    pick, pick_t = tables(block_offset)
    weight, weight_t = weights(tiles), weights(jnp.swapaxes(tiles, 1, 2))
    turned = vert.reshape(variables, levels_all, n_lev, levels).transpose(0, 3, 2, 1).reshape(vert.shape)
    own_root = lax.dynamic_slice_in_dim(static_vertical_root, lax.axis_index("mem") * deep, deep, 1)

    vmem, hbm = pltpu.VMEM, pltpu.HBM
    chunks = vmem((n_lev, rows, LANES), BF16)
    parts = vmem((n_mem, variables * deep, LANES), BF16)
    field = vmem((variables * deep, LANES), F32)
    kept = (rows, PAIRS, LANES)
    flat = vmem((n_lev * rows, LANES), F32)
    moved = vmem((n_lev * rows, slots * LANES), BF16)
    dma = pltpu.SemaphoreType.DMA
    flat_obs = lambda x: x.reshape(-1, LANES)
    across = lambda x, axis: lax.all_to_all(x, axis, 0, 0, tiled=True)

    send, held = call(
        forward_first,
        (chunks, hbm(kept, BF16)),
        (
            flat,
            moved,
            vmem((slots * BLOCKS, BLOCKS), BF16),
            vmem((slots * LANES, LANES), BF16),
            vmem(kept, BF16),
            vmem(control.shape, BF16),
            vmem((slots, BLOCKS), jnp.int32),
            vmem(tiles.shape, BF16),
            dma((members + 3,)),
        ),
        (control, block_offset.T, tiles),
        stay=(0, 1, 2),
    )
    slope, shift = call(
        observations,
        (field, field),
        (),
        (flat_obs(obs_index), flat_obs(obs_value), flat_obs(obs_sigma), flat_obs(huber_mask)),
    )
    root_t = jnp.swapaxes(static_vertical_root, 1, 2)
    recv, slope, shift, own_root, root_t, turned, pick, pick_t, weight, weight_t = lax.optimization_barrier(
        (across(send, "lev"), slope, shift, own_root, root_t, turned, pick, pick_t, weight, weight_t)
    )
    static = static_control_vector
    for turn in range(ITERS):
        partial = call(ensemble, parts, (flat,), (recv, perturb, turned))
        grad = call(
            gradient, parts, (), (across(partial, "mem"), static, own_root, slope, shift), gain=gain
        )
        grad = across(grad, "mem")
        send = call(backward, chunks, (flat,), (grad, perturb, turned), gain=gain)
        operands = (across(send, "lev"), held, pick_t, weight_t, grad, root_t, static)
        if turn + 1 < ITERS:
            send, held, static = call(
                backward_forward,
                (chunks, hbm(kept, BF16), hbm(static.shape, BF16)),
                (flat, moved, vmem(kept, BF16), vmem(static.shape, BF16), dma((2,))),
                (*operands, pick, weight),
            )
            recv = across(send, "lev")
        else:
            control, static = call(
                backward_last,
                (hbm(control.shape, BF16), hbm(static.shape, BF16)),
                (
                    flat,
                    moved,
                    vmem((rows * PAIRS, LANES), F32),
                    vmem(control.shape, BF16),
                    vmem(static.shape, BF16),
                    dma((members + 1,)),
                ),
                operands,
            )
    return (control, static)


def solution(mesh):
    placed = (
        P("mem", None, "lev", None),
        P(None, None, "lev"),
        P("mem", None, None, "lev"),
        P(),
        P(),
        P(),
        P(),
        P(("lev", "mem")),
        P(("lev", "mem")),
        P(("lev", "mem")),
        P(("lev", "mem")),
    )
    return jax.shard_map(
        on_device,
        mesh=mesh,
        in_specs=placed,
        out_specs=(P("mem", None, "lev", None), P(None, None, "lev")),
        check_vma=False,
    )
```

time: 213 us -> 186 us (0.87)
  blocking collectives: 96 us -> 133 us
  waiting for transfers between devices: 49.7 us -> 18.5 us
  Pallas kernels: 28 us -> 12.3 us
  starting transfers between devices: 28.7 us -> 16.7 us
  local copies, waits for them, and re-layouts: 6.47 us -> 3.95 us
    all_to_all x5 -> x7, blocking collectives: 96 us -> 133 us  [on_device(): across = lambda x, axis: lax.all_to_all(x, axis, 0, 0, tiled=True)]
    all_to_all x3 -> x1, waiting for transfers between devices: 49.7 us -> 18.5 us  [on_device(): across = lambda x, axis: lax.all_to_all(x, axis, 0, 0, tiled=True)]
    pallas_call x10, Pallas kernels: 28 us -> 12.3 us  [call(): run(*(a if i in stay else pltpu.with_memory_space_constraint(a, pltpu.VME...]
    all_to_all x3 -> x1, starting transfers between devices: 28.7 us -> 16.7 us  [on_device(): across = lambda x, axis: lax.all_to_all(x, axis, 0, 0, tiled=True)]
  transfers between devices with their start and end apart: 3 -> 1, of which waited for: 3 -> 1; matrix products, arithmetic and copies ran while one was open for 2% -> 1% of each run, Pallas kernels for 1% -> 0%
where the time goes in v3:
time: 186 us; the launch traced here: 185 us
  blocking collectives  133 us (72%)
  waiting for transfers between devices  18.5 us (10%)
  starting transfers between devices  16.7 us (9%)
  Pallas kernels  12.3 us (7%)
  local copies, waits for them, and re-layouts  3.95 us (2%)
    all_to_all x7, blocking collectives, on_device(): across = lambda x, axis: lax.all_to_all(x, axis, 0, 0, tiled=True)  133 us
    all_to_all x1, waiting for transfers between devices, on_device(): across = lambda x, axis: lax.all_to_all(x, axis, 0, 0, tiled=True)  18.5 us
    all_to_all x1, starting transfers between devices, on_device(): across = lambda x, axis: lax.all_to_all(x, axis, 0, 0, tiled=True)  16.7 us
    pallas_call x10, Pallas kernels, call(): run(*(a if i in stay else pltpu.with_memory_space_constraint(a, pltpu.VME...  12.3 us
  transfers between devices with their start and end apart: 1, of which 1 were waited for; matrix products, arithmetic and copies ran while one was open for 1% of the time, Pallas kernels for 0%

profile of v3, /device:TPU:2, one launch (start us, length us, event | category | flops | bytes accessed | tf_op | source)
XLA Modules:
  0.0 185.4 jit_solution(9068975398865556657)
XLA Ops:
  0.6 3.2 %forward_first.1 = (bf16[32,40,128]{2,1,0:T(8,128)(2,1)}, bf16[40,32,128]{2,1,0:T(8,128)(2,1)}) custom-call(bf16[2,5,4,4096]{3,2,1,0:T(4,128)(2,1)} %control_hbm.1, s32[4,64]{1,0:T(4,128)} %bitcast.44, bf16[4,64,64]{2,1,0:T(8,128)(2,1)} %tiles_hbm.1), custom_call_target="tpu_custom_call" | custom-call | tf_op jit(solution)/shard_map/forward_first/pallas_call | solution.py:35
  3.9 16.7 %all-to-all-start = ((bf16[32,40,128]{2,1,0:T(8,128)(2,1)}), bf16[32,40,128]{2,1,0:T(8,128)(2,1)S(1)}, u32[]{:S(2)}, u32[]{:S(2)}) async-start(bf16[32,40,128]{2,1,0:T(8,128)(2,1)} %get-tuple-element.19), calls=%async_computation | async-start | bytes 655360 | tf_op jit(solution)/shard_map/all_to_all | solution.py:383
  20.7 0.1 copy.20
  20.8 0.1 copy.21
  20.9 0.1 eq.40
  21.1 0.3 copy-done.9
  21.5 0.1 pad_bitcast_fusion.3
  21.6 0.9 copy-done.11
  22.5 0.2 copy.18
  22.7 0.9 copy-done.10
  23.6 0.2 copy.17
  23.9 0.1 copy.24
  24.1 0.1 fusion
  24.2 0.5 copy-done.6
  24.7 0.1 copy-done.5
  24.9 0.7 observations.1
  25.6 18.5 %all-to-all-done.recv_ref = bf16[32,40,128]{2,1,0:T(8,128)(2,1)S(1)} async-done(((bf16[32,40,128]{2,1,0:T(8,128)(2,1)}), bf16[32,40,128]{2,1,0:T(8,128)(2,1)S(1)}, u32[]{:S(2)}, u32[]{:S(2)}) %all-to-all-start) | async-done | bytes 327712 | tf_op jit(solution)/shard_map/all_to_all | solution.py:383
  44.2 0.3 ensemble.2
  44.5 14.6 %all_to_all.40.recv_ref = bf16[16,40,128]{2,1,0:T(8,128)(2,1)S(1)} all-to-all(bf16[16,40,128]{2,1,0:T(8,128)(2,1)S(1)} %ensemble.2), channel_id=1, replica_groups=mesh['lev'=32,'mem'=16] {'mem'}, dimensions={0} | all-to-all | bytes 327680 | tf_op jit(solution)/shard_map/all_to_all | solution.py:383
  59.1 0.2 gradient.2
  59.2 11.1 %all_to_all.41.recv_ref.grad_ref = bf16[16,40,128]{2,1,0:T(8,128)(2,1)S(1)} all-to-all(bf16[16,40,128]{2,1,0:T(8,128)(2,1)S(1)} %gradient.2), channel_id=1, replica_groups=mesh['lev'=32,'mem'=16] {'mem'}, dimensions={0} | all-to-all | bytes 327680 | tf_op jit(solution)/shard_map/all_to_all | solution.py:383
  70.4 0.4 backward.2
  70.8 28.7 %all_to_all.42.recv_ref = bf16[32,40,128]{2,1,0:T(8,128)(2,1)S(1)} all-to-all(bf16[32,40,128]{2,1,0:T(8,128)(2,1)S(1)} %backward.2), channel_id=1, replica_groups=mesh['lev'=32,'mem'=16] {'lev'}, dimensions={0} | all-to-all | bytes 655360 | tf_op jit(solution)/shard_map/all_to_all | solution.py:383
  99.5 3.6 %backward_forward.1 = (bf16[32,40,128]{2,1,0:T(8,128)(2,1)S(1)}, bf16[40,32,128]{2,1,0:T(8,128)(2,1)}, bf16[5,128,128]{2,1,0:T(8,128)(2,1)}) custom-call(bf16[32,40,128]{2,1,0:T(8,128)(2,1)S(1)} %all_to_all.42.recv_ref, bf16[40,32,128]{2,1,0:T(8,128)(2,1)S(1)} %copy-done.3, bf16[256,64]{1,0:T(8,128)(2,1)S(1)} %get-tuple-element.28.pick_t_ref, ...), custom_call_target="tpu_custom_call" | custom-call | tf_op jit(solution)/shard_map/backward_forward/pallas_call | solution.py:35
  103.1 27.9 %all_to_all.43.recv_ref = bf16[32,40,128]{2,1,0:T(8,128)(2,1)S(1)} all-to-all(bf16[32,40,128]{2,1,0:T(8,128)(2,1)S(1)} %get-tuple-element.33), channel_id=1, replica_groups=mesh['lev'=32,'mem'=16] {'lev'}, dimensions={0} | all-to-all | bytes 655360 | tf_op jit(solution)/shard_map/all_to_all | solution.py:383
  131.0 0.3 ensemble.3
  131.3 11.3 %all_to_all.44.recv_ref = bf16[16,40,128]{2,1,0:T(8,128)(2,1)S(1)} all-to-all(bf16[16,40,128]{2,1,0:T(8,128)(2,1)S(1)} %ensemble.3), channel_id=1, replica_groups=mesh['lev'=32,'mem'=16] {'mem'}, dimensions={0} | all-to-all | bytes 327680 | tf_op jit(solution)/shard_map/all_to_all | solution.py:383
  142.6 0.2 gradient.3
  142.7 11.1 %all_to_all.45.recv_ref.grad_ref = bf16[16,40,128]{2,1,0:T(8,128)(2,1)S(1)} all-to-all(bf16[16,40,128]{2,1,0:T(8,128)(2,1)S(1)} %gradient.3), channel_id=1, replica_groups=mesh['lev'=32,'mem'=16] {'mem'}, dimensions={0} | all-to-all | bytes 327680 | tf_op jit(solution)/shard_map/all_to_all | solution.py:383
  153.8 0.4 backward.3
  154.2 28.1 %all_to_all.46.recv_ref = bf16[32,40,128]{2,1,0:T(8,128)(2,1)S(1)} all-to-all(bf16[32,40,128]{2,1,0:T(8,128)(2,1)S(1)} %backward.3), channel_id=1, replica_groups=mesh['lev'=32,'mem'=16] {'lev'}, dimensions={0} | all-to-all | bytes 655360 | tf_op jit(solution)/shard_map/all_to_all | solution.py:383
  182.3 3.1 %backward_last.1 = (bf16[2,5,4,4096]{3,2,1,0:T(4,128)(2,1)}, bf16[5,128,128]{2,1,0:T(8,128)(2,1)}) custom-call(bf16[32,40,128]{2,1,0:T(8,128)(2,1)S(1)} %all_to_all.46.recv_ref, bf16[40,32,128]{2,1,0:T(8,128)(2,1)S(1)} %copy-done.4, bf16[256,64]{1,0:T(8,128)(2,1)S(1)} %get-tuple-element.28.pick_t_ref, bf16[512,128]{1,0:T(8,128)(2,1)S(1)} %bitcast.35, ...), custom_call_target="tpu_custom_call" | custom-call | tf_op jit(solution)/shard_map/backward_last/pallas_call | solution.py:35
  (31 shorter events, 0.4 us)
Async XLA Ops:
  3.9 16.8 %copy-start.12 = (s32[64,4]{0,1:T(4,128)S(1)}, s32[64,4]{0,1:T(4,128)}, u32[]{:S(2)}) copy-start(s32[64,4]{0,1:T(4,128)} %param.15) | copy-start | bytes 3076
  3.9 40.3 %all-to-all-start = ((bf16[32,40,128]{2,1,0:T(8,128)(2,1)}), bf16[32,40,128]{2,1,0:T(8,128)(2,1)S(1)}, u32[]{:S(2)}, u32[]{:S(2)}) async-start(bf16[32,40,128]{2,1,0:T(8,128)(2,1)} %get-tuple-element.19), calls=%async_computation | async-start | bytes 655360 | tf_op jit(solution)/shard_map/all_to_all | solution.py:383
  20.6 0.8 copy-start.9
  21.6 0.9 copy-start.11
  22.7 0.9 copy-start.10
  23.9 20.3 %copy-start = (bf16[2,5,128,128]{3,2,1,0:T(8,128)(2,1)S(1)}, bf16[2,5,128,128]{3,2,1,0:T(8,128)(2,1)}, u32[]{:S(2)}) copy-start(bf16[2,5,128,128]{3,2,1,0:T(8,128)(2,1)} %perturb_ref.7) | copy-start | bytes 983044
  24.0 0.7 copy-start.6
  24.0 0.7 copy-start.7
  24.0 0.7 copy-start.8
  24.2 0.7 copy-start.5
  44.4 14.6 %copy-start.1 = (bf16[5,128,128]{2,1,0:T(8,128)(2,1)S(1)}, bf16[5,128,128]{2,1,0:T(8,128)(2,1)}, u32[]{:S(2)}) copy-start(bf16[5,128,128]{2,1,0:T(8,128)(2,1)} %static_ref.3) | copy-start | bytes 491524
  70.7 28.7 %copy-start.3 = (bf16[40,32,128]{2,1,0:T(8,128)(2,1)S(1)}, bf16[40,32,128]{2,1,0:T(8,128)(2,1)}, u32[]{:S(2)}) copy-start(bf16[40,32,128]{2,1,0:T(8,128)(2,1)} %get-tuple-element.27.kept_ref) | copy-start | bytes 983044
  131.3 11.3 %copy-start.2 = (bf16[5,128,128]{2,1,0:T(8,128)(2,1)S(1)}, bf16[5,128,128]{2,1,0:T(8,128)(2,1)}, u32[]{:S(2)}) copy-start(bf16[5,128,128]{2,1,0:T(8,128)(2,1)} %get-tuple-element.34.static_ref) | copy-start | bytes 491524
  154.2 28.1 %copy-start.4 = (bf16[40,32,128]{2,1,0:T(8,128)(2,1)S(1)}, bf16[40,32,128]{2,1,0:T(8,128)(2,1)}, u32[]{:S(2)}) copy-start(bf16[40,32,128]{2,1,0:T(8,128)(2,1)} %get-tuple-element.35.kept_ref) | copy-start | bytes 983044

commit v4 on v3

--- a/solution.py
+++ b/solution.py
@@ -73,6 +73,31 @@
             store(2 * (g + p) + 1, y)
 
 
+def gather(load, loaded, source, send_ref, weight_ref, halves, moved):
+    count, rows = send_ref.shape[:2]
+    low = iota((rows, LANES), 1) < HALF
+    for j in range(count):
+        x = load(j)
+        y = pltpu.roll(x, HALF, 1)
+        halves[2 * j, :rows] = jnp.where(low, x, 0.0).astype(BF16)
+        halves[2 * j + 1, :rows] = jnp.where(low, y, 0.0).astype(BF16)
+        halves[BLOCKS + 2 * j, :rows] = jnp.where(low, 0.0, y).astype(BF16)
+        halves[BLOCKS + 2 * j + 1, :rows] = jnp.where(low, 0.0, x).astype(BF16)
+    loaded()
+    deep = moved.shape[0] // count
+    for j in range(count):
+        for h in range(2):
+            for k in range(0, weight_ref.shape[0] // LANES, 2):
+                both = halves[source(k, 2 * j + h), :rows] + halves[BLOCKS + source(k + 1, 2 * j + h), :rows]
+                at = (h * (weight_ref.shape[0] // LANES) + k) // 2
+                moved[pl.ds(j * deep, rows), pl.ds(at * LANES, LANES)] = both
+    some = count // 2
+    for g in range(0, count, some):
+        out = dot(moved[pl.ds(g * deep, some * deep), :], weight_ref[...])
+        for i in range(some):
+            send_ref[g + i] = out[i * deep : i * deep + rows].astype(BF16)
+
+
 def open_chunks(recv_ref, flat):
     rows = recv_ref.shape[1]
     for j in range(recv_ref.shape[0]):
@@ -105,10 +130,10 @@
     kept_hbm,
     flat,
     moved,
-    pick,
     weight,
     kept,
     control,
+    halves,
     offset_ref,
     tiles_ref,
     sems,
@@ -120,23 +145,15 @@
         pltpu.make_async_copy(offset_hbm, offset_ref, sems.at[members + 1]),
         pltpu.make_async_copy(tiles_hbm, tiles_ref, sems.at[members + 2]),
     ]
-    for copy in small + fetch:
+    for copy in fetch + small:
         copy.start()
-    for copy in small:
-        copy.wait()
-    square = (BLOCKS, BLOCKS)
-    block = iota(square, 1)
-    turn = ones(iota(square, 0) == (block & 1) * PAIRS + (block >> 1))
+    small[1].wait()
     wide = (HALF, LANES)
-    left, right = ones(iota(wide, 1) == iota(wide, 0)), ones(iota(wide, 1) == iota(wide, 0) + HALF)
-    for k in range(tiles_ref.shape[0]):
-        source = (block[:1] + offset_ref[k : k + 1, :]) & (BLOCKS - 1)
-        spot = (source & 1) * PAIRS + (source >> 1)
-        found = ones(iota(square, 0) == spot)
-        pick[pl.ds(k * BLOCKS, BLOCKS), :] = dot(turn, found, ((1,), (1,))).astype(BF16)
-        tile = tiles_ref[k]
-        weight[pl.ds(2 * k * HALF, HALF), :] = dot(tile, left).astype(BF16)
-        weight[pl.ds((2 * k + 1) * HALF, HALF), :] = dot(tile, right).astype(BF16)
+    places = ones(iota(wide, 1) == iota(wide, 0)), ones(iota(wide, 1) == iota(wide, 0) + HALF)
+    slots = tiles_ref.shape[0]
+    for h, place in enumerate(places):
+        for k in range(slots):
+            weight[pl.ds((h * slots + k) * HALF, HALF), :] = dot(tiles_ref[k], place).astype(BF16)
     for m in range(members):
         fetch[m].wait()
         for v in range(variables):
@@ -145,17 +162,15 @@
             for j in range(columns // LANES):
                 flat[pl.ds(j * rows + at, levels), :] = x[:, j * LANES : (j + 1) * LANES]
 
-    load, store = by_row(flat, rows)
-
-    def load_kept(r):
-        x = load(r)
-        kept[r] = x.astype(BF16)
+    def load(j):
+        x = flat[pl.ds(j * rows, rows), :]
+        kept[j] = x.astype(BF16)
         return x
 
     keep = pltpu.make_async_copy(kept, kept_hbm, sems.at[members])
-    spread(load_kept, store, pick, weight, moved)
-    keep.start()
-    close_chunks(flat, send_ref)
+    small[0].wait()
+    source = lambda k, b: (b + offset_ref[k, b]) & (BLOCKS - 1)
+    gather(load, keep.start, source, send_ref, weight, halves, moved)
     keep.wait()
 
 
@@ -180,7 +195,7 @@
     grad_ref,
     root_ref,
     static_ref,
-    pick_ref,
+    source_hbm,
     weight_ref,
     send_ref,
     next_hbm,
@@ -189,23 +204,30 @@
     moved,
     next_ref,
     moving_ref,
+    halves,
+    moved_ahead,
+    source_ref,
     sems,
 ):
+    fetch = pltpu.make_async_copy(source_hbm, source_ref, sems.at[2])
+    fetch.start()
     descend_static(grad_ref, root_ref, static_ref, moving_ref)
     keep_static = pltpu.make_async_copy(moving_ref, moving_hbm, sems.at[0])
     keep_static.start()
-    load, store = by_row(flat, recv_ref.shape[1])
+    rows = recv_ref.shape[1]
+    load, store = by_row(flat, rows)
     open_chunks(recv_ref, flat)
-
-    def update(r, adjoint):
-        current = kept_ref[r].astype(F32)
-        next_ref[r] = (current - TAU * (current + adjoint)).astype(BF16)
+    spread(load, store, pick_t_ref, weight_t_ref, moved)
+
+    def update(j):
+        current = kept_ref[j].astype(F32)
+        x = (current - TAU * (current + flat[pl.ds(j * rows, rows), :])).astype(BF16)
+        next_ref[j] = x
+        return x.astype(F32)
 
     keep = pltpu.make_async_copy(next_ref, next_hbm, sems.at[1])
-    spread(load, update, pick_t_ref, weight_t_ref, moved)
-    keep.start()
-    spread(lambda r: next_ref[r].astype(F32), store, pick_ref, weight_ref, moved)
-    close_chunks(flat, send_ref)
+    fetch.wait()
+    gather(update, keep.start, lambda k, b: source_ref[k, b], send_ref, weight_ref, halves, moved_ahead)
     keep_static.wait()
     keep.wait()
 
@@ -231,20 +253,19 @@
     descend_static(grad_ref, root_ref, static_ref, moving_ref)
     keep_static = pltpu.make_async_copy(moving_ref, moving_hbm, sems.at[members])
     keep_static.start()
-    load, _ = by_row(flat, recv_ref.shape[1])
+    rows = recv_ref.shape[1]
+    load, store = by_row(flat, rows)
     open_chunks(recv_ref, flat)
-
-    def update(r, adjoint):
-        current = kept_ref[r].astype(F32)
-        final[pl.ds(r * PAIRS, PAIRS), :] = current - TAU * (current + adjoint)
-
-    spread(load, update, pick_t_ref, weight_t_ref, moved)
+    spread(load, store, pick_t_ref, weight_t_ref, moved)
+    for j in range(columns // LANES):
+        current = kept_ref[j].astype(F32)
+        final[pl.ds(j * rows, rows), :] = current - TAU * (current + flat[pl.ds(j * rows, rows), :])
     copies = [pltpu.make_async_copy(control.at[m], control_hbm.at[m], sems.at[m]) for m in range(members)]
     for m in range(members):
         for v in range(variables):
-            start = (m * variables + v) * levels * PAIRS
+            at = (m * variables + v) * levels
             for j in range(columns // LANES):
-                x = final[pl.ds(start + j, levels, stride=PAIRS), :]
+                x = final[pl.ds(j * rows + at, levels), :]
                 control[m, v, :, pl.ds(j * LANES, LANES)] = x.astype(BF16)
         copies[m].start()
     keep_static.wait()
@@ -333,16 +354,15 @@
     source = (blocks[:, None] + block_offset) % count
     spot = (source % 2) * (count // 2) + source // 2
     by_slot = spot.reshape(count // 2, 2, slots).transpose(2, 1, 0)
-    forth = by_slot.reshape(-1, 1) == blocks[None, :]
     back = (by_slot.reshape(slots, 1, count) == blocks[None, :, None]).reshape(slots * count, count)
-    return forth.astype(BF16), back.astype(BF16)
+    return source.T, back.astype(BF16)
 
 
 def weights(tiles):
-    slots, width = tiles.shape[:2]
+    width = tiles.shape[1]
     left = jnp.pad(tiles, ((0, 0), (0, 0), (0, width)))
     right = jnp.pad(tiles, ((0, 0), (0, 0), (width, 0)))
-    return jnp.stack([left, right], axis=1).reshape(slots * 2 * width, 2 * width)
+    return left, right
 
 
 def on_device(
@@ -366,8 +386,9 @@
     slots = tiles.shape[0]
     gain = ENS_W / math.sqrt(members * n_mem)
 
-    pick, pick_t = tables(block_offset)
-    weight, weight_t = weights(tiles), weights(jnp.swapaxes(tiles, 1, 2))
+    source, pick_t = tables(block_offset)
+    weight = jnp.concatenate(weights(tiles), axis=0).reshape(-1, LANES)
+    weight_t = jnp.stack(weights(jnp.swapaxes(tiles, 1, 2)), axis=1).reshape(-1, LANES)
     turned = vert.reshape(variables, levels_all, n_lev, levels).transpose(0, 3, 2, 1).reshape(vert.shape)
     own_root = lax.dynamic_slice_in_dim(static_vertical_root, lax.axis_index("mem") * deep, deep, 1)
 
@@ -375,7 +396,10 @@
     chunks = vmem((n_lev, rows, LANES), BF16)
     parts = vmem((n_mem, variables * deep, LANES), BF16)
     field = vmem((variables * deep, LANES), F32)
-    kept = (rows, PAIRS, LANES)
+    kept = (PAIRS, rows, LANES)
+    padded = -(-rows // 16) * 16
+    halves = vmem((2 * BLOCKS, padded, LANES), BF16)
+    moved_ahead = vmem((PAIRS * padded, slots * LANES), BF16)
     flat = vmem((n_lev * rows, LANES), F32)
     moved = vmem((n_lev * rows, slots * LANES), BF16)
     dma = pltpu.SemaphoreType.DMA
@@ -387,12 +411,12 @@
         (chunks, hbm(kept, BF16)),
         (
             flat,
-            moved,
-            vmem((slots * BLOCKS, BLOCKS), BF16),
+            moved_ahead,
             vmem((slots * LANES, LANES), BF16),
             vmem(kept, BF16),
             vmem(control.shape, BF16),
-            vmem((slots, BLOCKS), jnp.int32),
+            halves,
+            pltpu.SMEM((slots, BLOCKS), jnp.int32),
             vmem(tiles.shape, BF16),
             dma((members + 3,)),
         ),
@@ -406,8 +430,8 @@
         (flat_obs(obs_index), flat_obs(obs_value), flat_obs(obs_sigma), flat_obs(huber_mask)),
     )
     root_t = jnp.swapaxes(static_vertical_root, 1, 2)
-    recv, slope, shift, own_root, root_t, turned, pick, pick_t, weight, weight_t = lax.optimization_barrier(
-        (across(send, "lev"), slope, shift, own_root, root_t, turned, pick, pick_t, weight, weight_t)
+    recv, slope, shift, own_root, root_t, turned, source, pick_t, weight, weight_t = lax.optimization_barrier(
+        (across(send, "lev"), slope, shift, own_root, root_t, turned, source, pick_t, weight, weight_t)
     )
     static = static_control_vector
     for turn in range(ITERS):
@@ -422,8 +446,18 @@
             send, held, static = call(
                 backward_forward,
                 (chunks, hbm(kept, BF16), hbm(static.shape, BF16)),
-                (flat, moved, vmem(kept, BF16), vmem(static.shape, BF16), dma((2,))),
-                (*operands, pick, weight),
+                (
+                    flat,
+                    moved,
+                    vmem(kept, BF16),
+                    vmem(static.shape, BF16),
+                    halves,
+                    moved_ahead,
+                    pltpu.SMEM((slots, BLOCKS), jnp.int32),
+                    dma((3,)),
+                ),
+                (*operands, source, weight),
+                stay=(7,),
             )
             recv = across(send, "lev")
         else:
@@ -433,7 +467,7 @@
                 (
                     flat,
                     moved,
-                    vmem((rows * PAIRS, LANES), F32),
+                    flat,
                     vmem(control.shape, BF16),
                     vmem(static.shape, BF16),
                     dma((members + 1,)),

time: 186 us -> 186 us (level)
  no operation moved by 1% of the time
where the time goes in v4:
time: 186 us; the launch traced here: 185 us
  blocking collectives  133 us (72%)
  waiting for transfers between devices  18.2 us (10%)
  starting transfers between devices  16.9 us (9%)
  Pallas kernels  12.1 us (7%)
  local copies, waits for them, and re-layouts  3.78 us (2%)
    all_to_all x7, blocking collectives, on_device(): across = lambda x, axis: lax.all_to_all(x, axis, 0, 0, tiled=True)  133 us
    all_to_all x1, waiting for transfers between devices, on_device(): across = lambda x, axis: lax.all_to_all(x, axis, 0, 0, tiled=True)  18.2 us
    all_to_all x1, starting transfers between devices, on_device(): across = lambda x, axis: lax.all_to_all(x, axis, 0, 0, tiled=True)  16.9 us
    pallas_call x10, Pallas kernels, call(): run(*(a if i in stay else pltpu.with_memory_space_constraint(a, pltpu.VME...  12.1 us
  transfers between devices with their start and end apart: 1, of which 1 were waited for; matrix products, arithmetic and copies ran while one was open for 1% of the time, Pallas kernels for 0%

profile of v4, /device:TPU:2, one launch (start us, length us, event | category | flops | bytes accessed | tf_op | source)
XLA Modules:
  0.0 185.3 jit_solution(15288908454115932005)
XLA Ops:
  0.6 3.3 %forward_first.1 = (bf16[32,40,128]{2,1,0:T(8,128)(2,1)}, bf16[32,40,128]{2,1,0:T(8,128)(2,1)}) custom-call(bf16[2,5,4,4096]{3,2,1,0:T(4,128)(2,1)} %control_hbm.1, s32[4,64]{1,0:T(4,128)} %bitcast.42, bf16[4,64,64]{2,1,0:T(8,128)(2,1)} %tiles_hbm.1), custom_call_target="tpu_custom_call" | custom-call | tf_op jit(solution)/shard_map/forward_first/pallas_call | solution.py:35
  3.9 16.9 %all-to-all-start = ((bf16[32,40,128]{2,1,0:T(8,128)(2,1)}), bf16[32,40,128]{2,1,0:T(8,128)(2,1)S(1)}, u32[]{:S(2)}, u32[]{:S(2)}) async-start(bf16[32,40,128]{2,1,0:T(8,128)(2,1)} %get-tuple-element.19), calls=%async_computation | async-start | bytes 655360 | tf_op jit(solution)/shard_map/all_to_all | solution.py:407
  20.9 0.6 copy-done.12
  21.5 0.6 fusion.6
  22.0 0.1 copy.19
  22.1 0.1 copy.20
  22.3 0.2 copy.17
  22.5 0.9 copy-done.10
  23.4 0.2 copy.16
  23.6 0.7 copy-done.9
  24.3 0.1 copy.21
  24.5 0.1 fusion.3.pick_t_ref
  24.6 0.5 copy-done.6
  25.2 0.1 copy-done.5
  25.3 0.7 observations.1
  26.0 0.1 fusion.2
  26.1 18.2 %all-to-all-done.recv_ref = bf16[32,40,128]{2,1,0:T(8,128)(2,1)S(1)} async-done(((bf16[32,40,128]{2,1,0:T(8,128)(2,1)}), bf16[32,40,128]{2,1,0:T(8,128)(2,1)S(1)}, u32[]{:S(2)}, u32[]{:S(2)}) %all-to-all-start) | async-done | bytes 327712 | tf_op jit(solution)/shard_map/all_to_all | solution.py:407
  44.3 0.3 ensemble.2
  44.6 14.6 %all_to_all.40.recv_ref = bf16[16,40,128]{2,1,0:T(8,128)(2,1)S(1)} all-to-all(bf16[16,40,128]{2,1,0:T(8,128)(2,1)S(1)} %ensemble.2), channel_id=1, replica_groups=mesh['lev'=32,'mem'=16] {'mem'}, dimensions={0} | all-to-all | bytes 327680 | tf_op jit(solution)/shard_map/all_to_all | solution.py:407
  59.2 0.2 gradient.2
  59.4 11.1 %all_to_all.41.recv_ref.grad_ref = bf16[16,40,128]{2,1,0:T(8,128)(2,1)S(1)} all-to-all(bf16[16,40,128]{2,1,0:T(8,128)(2,1)S(1)} %gradient.2), channel_id=1, replica_groups=mesh['lev'=32,'mem'=16] {'mem'}, dimensions={0} | all-to-all | bytes 327680 | tf_op jit(solution)/shard_map/all_to_all | solution.py:407
  70.5 0.4 backward.2
  70.9 28.7 %all_to_all.42.recv_ref = bf16[32,40,128]{2,1,0:T(8,128)(2,1)S(1)} all-to-all(bf16[32,40,128]{2,1,0:T(8,128)(2,1)S(1)} %backward.2), channel_id=1, replica_groups=mesh['lev'=32,'mem'=16] {'lev'}, dimensions={0} | all-to-all | bytes 655360 | tf_op jit(solution)/shard_map/all_to_all | solution.py:407
  99.6 3.5 %backward_forward.1 = (bf16[32,40,128]{2,1,0:T(8,128)(2,1)S(1)}, bf16[32,40,128]{2,1,0:T(8,128)(2,1)}, bf16[5,128,128]{2,1,0:T(8,128)(2,1)}) custom-call(bf16[32,40,128]{2,1,0:T(8,128)(2,1)S(1)} %all_to_all.42.recv_ref, bf16[32,40,128]{2,1,0:T(8,128)(2,1)S(1)} %copy-done.3, bf16[256,64]{1,0:T(8,128)(2,1)S(1)} %fusion.3.pick_t_ref, ...), custom_call_target="tpu_custom_call" | custom-call | tf_op jit(solution)/shard_map/backward_forward/pallas_call | solution.py:35
  103.2 27.9 %all_to_all.43.recv_ref = bf16[32,40,128]{2,1,0:T(8,128)(2,1)S(1)} all-to-all(bf16[32,40,128]{2,1,0:T(8,128)(2,1)S(1)} %get-tuple-element.33), channel_id=1, replica_groups=mesh['lev'=32,'mem'=16] {'lev'}, dimensions={0} | all-to-all | bytes 655360 | tf_op jit(solution)/shard_map/all_to_all | solution.py:407
  131.0 0.3 ensemble.3
  131.3 11.3 %all_to_all.44.recv_ref = bf16[16,40,128]{2,1,0:T(8,128)(2,1)S(1)} all-to-all(bf16[16,40,128]{2,1,0:T(8,128)(2,1)S(1)} %ensemble.3), channel_id=1, replica_groups=mesh['lev'=32,'mem'=16] {'mem'}, dimensions={0} | all-to-all | bytes 327680 | tf_op jit(solution)/shard_map/all_to_all | solution.py:407
  142.6 0.2 gradient.3
  142.8 11.1 %all_to_all.45.recv_ref.grad_ref = bf16[16,40,128]{2,1,0:T(8,128)(2,1)S(1)} all-to-all(bf16[16,40,128]{2,1,0:T(8,128)(2,1)S(1)} %gradient.3), channel_id=1, replica_groups=mesh['lev'=32,'mem'=16] {'mem'}, dimensions={0} | all-to-all | bytes 327680 | tf_op jit(solution)/shard_map/all_to_all | solution.py:407
  153.9 0.4 backward.3
  154.3 28.1 %all_to_all.46.recv_ref = bf16[32,40,128]{2,1,0:T(8,128)(2,1)S(1)} all-to-all(bf16[32,40,128]{2,1,0:T(8,128)(2,1)S(1)} %backward.3), channel_id=1, replica_groups=mesh['lev'=32,'mem'=16] {'lev'}, dimensions={0} | all-to-all | bytes 655360 | tf_op jit(solution)/shard_map/all_to_all | solution.py:407
  182.4 2.9 %backward_last.1 = (bf16[2,5,4,4096]{3,2,1,0:T(4,128)(2,1)}, bf16[5,128,128]{2,1,0:T(8,128)(2,1)}) custom-call(bf16[32,40,128]{2,1,0:T(8,128)(2,1)S(1)} %all_to_all.46.recv_ref, bf16[32,40,128]{2,1,0:T(8,128)(2,1)S(1)} %copy-done.4, bf16[256,64]{1,0:T(8,128)(2,1)S(1)} %fusion.3.pick_t_ref, bf16[512,128]{1,0:T(8,128)(2,1)S(1)} %bitcast.33, ...), custom_call_target="tpu_custom_call" | custom-call | tf_op jit(solution)/shard_map/backward_last/pallas_call | solution.py:35
  (28 shorter events, 0.4 us)
Async XLA Ops:
  3.9 18.4 %copy-start.11 = (bf16[5,128,128]{2,1,0:T(8,128)(2,1)S(1)}, bf16[5,128,128]{2,1,0:T(8,128)(2,1)}, u32[]{:S(2)}) copy-start(bf16[5,128,128]{2,1,0:T(8,128)(2,1)} %param.16) | copy-start | bytes 491524
  3.9 40.4 %all-to-all-start = ((bf16[32,40,128]{2,1,0:T(8,128)(2,1)}), bf16[32,40,128]{2,1,0:T(8,128)(2,1)S(1)}, u32[]{:S(2)}, u32[]{:S(2)}) async-start(bf16[32,40,128]{2,1,0:T(8,128)(2,1)} %get-tuple-element.19), calls=%async_computation | async-start | bytes 655360 | tf_op jit(solution)/shard_map/all_to_all | solution.py:407
  20.8 0.7 copy-start.12
  22.5 0.9 copy-start.10
  23.4 0.8 copy-start.9
  24.3 20.0 %copy-start = (bf16[2,5,128,128]{3,2,1,0:T(8,128)(2,1)S(1)}, bf16[2,5,128,128]{3,2,1,0:T(8,128)(2,1)}, u32[]{:S(2)}) copy-start(bf16[2,5,128,128]{3,2,1,0:T(8,128)(2,1)} %perturb_ref.7) | copy-start | bytes 983044
  24.5 0.7 copy-start.6
  24.5 0.7 copy-start.7
  24.5 0.7 copy-start.8
  24.6 0.7 copy-start.5
  44.6 14.6 %copy-start.1 = (bf16[5,128,128]{2,1,0:T(8,128)(2,1)S(1)}, bf16[5,128,128]{2,1,0:T(8,128)(2,1)}, u32[]{:S(2)}) copy-start(bf16[5,128,128]{2,1,0:T(8,128)(2,1)} %static_ref.3) | copy-start | bytes 491524
  70.9 28.7 %copy-start.3 = (bf16[32,40,128]{2,1,0:T(8,128)(2,1)S(1)}, bf16[32,40,128]{2,1,0:T(8,128)(2,1)}, u32[]{:S(2)}) copy-start(bf16[32,40,128]{2,1,0:T(8,128)(2,1)} %get-tuple-element.27.kept_ref) | copy-start | bytes 983044
  131.3 11.3 %copy-start.2 = (bf16[5,128,128]{2,1,0:T(8,128)(2,1)S(1)}, bf16[5,128,128]{2,1,0:T(8,128)(2,1)}, u32[]{:S(2)}) copy-start(bf16[5,128,128]{2,1,0:T(8,128)(2,1)} %get-tuple-element.34.static_ref) | copy-start | bytes 491524
  154.3 28.1 %copy-start.4 = (bf16[32,40,128]{2,1,0:T(8,128)(2,1)S(1)}, bf16[32,40,128]{2,1,0:T(8,128)(2,1)}, u32[]{:S(2)}) copy-start(bf16[32,40,128]{2,1,0:T(8,128)(2,1)} %get-tuple-element.35.kept_ref) | copy-start | bytes 983044

commit v5 on v4

--- a/solution.py
+++ b/solution.py
@@ -21,6 +21,7 @@
 HALF = 64
 PAIRS = 32
 BLOCKS = 64
+STAGGER_NS = 6500
 GROUP = 5
 
 
@@ -330,7 +331,7 @@
         send_ref[d] = grad
 
 
-def backward(recv_ref, perturb_ref, vert_ref, send_ref, flat, *, gain):
+def backward(recv_ref, perturb_ref, vert_ref, send_ref, flat, *, gain, hold):
     members, variables = perturb_ref.shape[:2]
     rows = send_ref.shape[1]
     levels = rows // (members * variables)
@@ -346,6 +347,11 @@
             for i in range(levels):
                 store(start + i, back[i * PAIRS : (i + 1) * PAIRS])
     close_chunks(flat, send_ref)
+    if hold:
+
+        @pl.when((lax.axis_index("mem") & 1) == 0)
+        def _():
+            pl.delay(hold)
 
 
 def tables(block_offset):
@@ -440,7 +446,7 @@
             gradient, parts, (), (across(partial, "mem"), static, own_root, slope, shift), gain=gain
         )
         grad = across(grad, "mem")
-        send = call(backward, chunks, (flat,), (grad, perturb, turned), gain=gain)
+        send = call(backward, chunks, (flat,), (grad, perturb, turned), gain=gain, hold=STAGGER_NS * (turn + 1 < ITERS))
         operands = (across(send, "lev"), held, pick_t, weight_t, grad, root_t, static)
         if turn + 1 < ITERS:
             send, held, static = call(

time: 186 us -> 181 us (0.973)
  blocking collectives: 133 us -> 128 us
    all_to_all x7, blocking collectives: 133 us -> 128 us  [on_device(): across = lambda x, axis: lax.all_to_all(x, axis, 0, 0, tiled=True)]
where the time goes in v5:
time: 181 us
  blocking collectives  128 us (71%)
  waiting for transfers between devices  18.2 us (10%)
  starting transfers between devices  16.9 us (9%)
  Pallas kernels  12.1 us (7%)
  local copies, waits for them, and re-layouts  3.78 us (2%)
    all_to_all x7, blocking collectives, on_device(): across = lambda x, axis: lax.all_to_all(x, axis, 0, 0, tiled=True)  128 us
    all_to_all x1, waiting for transfers between devices, on_device(): across = lambda x, axis: lax.all_to_all(x, axis, 0, 0, tiled=True)  18.2 us
    all_to_all x1, starting transfers between devices, on_device(): across = lambda x, axis: lax.all_to_all(x, axis, 0, 0, tiled=True)  16.9 us
    pallas_call x10, Pallas kernels, call(): run(*(a if i in stay else pltpu.with_memory_space_constraint(a, pltpu.VME...  12.1 us
  transfers between devices with their start and end apart: 1, of which 1 were waited for; matrix products, arithmetic and copies ran while one was open for 1% of the time, Pallas kernels for 0%

profile of v5, /device:TPU:2, one launch (start us, length us, event | category | flops | bytes accessed | tf_op | source)
XLA Modules:
  0.0 180.6 jit_solution(6077250962052928177)
XLA Ops:
  0.6 3.3 %forward_first.1 = (bf16[32,40,128]{2,1,0:T(8,128)(2,1)}, bf16[32,40,128]{2,1,0:T(8,128)(2,1)}) custom-call(bf16[2,5,4,4096]{3,2,1,0:T(4,128)(2,1)} %control_hbm.1, s32[4,64]{1,0:T(4,128)} %bitcast.42, bf16[4,64,64]{2,1,0:T(8,128)(2,1)} %tiles_hbm.1), custom_call_target="tpu_custom_call" | custom-call | tf_op jit(solution)/shard_map/forward_first/pallas_call | solution.py:36
  3.9 16.9 %all-to-all-start = ((bf16[32,40,128]{2,1,0:T(8,128)(2,1)}), bf16[32,40,128]{2,1,0:T(8,128)(2,1)S(1)}, u32[]{:S(2)}, u32[]{:S(2)}) async-start(bf16[32,40,128]{2,1,0:T(8,128)(2,1)} %get-tuple-element.19), calls=%async_computation | async-start | bytes 655360 | tf_op jit(solution)/shard_map/all_to_all | solution.py:413
  20.9 0.6 copy-done.12
  21.5 0.6 fusion.6
  22.0 0.1 copy.19
  22.1 0.1 copy.20
  22.3 0.2 copy.17
  22.5 0.9 copy-done.10
  23.4 0.2 copy.16
  23.6 0.7 copy-done.9
  24.3 0.1 copy.21
  24.5 0.1 fusion.3.pick_t_ref
  24.6 0.5 copy-done.6
  25.2 0.1 copy-done.5
  25.3 0.7 observations.1
  26.0 0.1 fusion.2
  26.1 18.2 %all-to-all-done.recv_ref = bf16[32,40,128]{2,1,0:T(8,128)(2,1)S(1)} async-done(((bf16[32,40,128]{2,1,0:T(8,128)(2,1)}), bf16[32,40,128]{2,1,0:T(8,128)(2,1)S(1)}, u32[]{:S(2)}, u32[]{:S(2)}) %all-to-all-start) | async-done | bytes 327712 | tf_op jit(solution)/shard_map/all_to_all | solution.py:413
  44.3 0.3 ensemble.2
  44.6 14.6 %all_to_all.40.recv_ref = bf16[16,40,128]{2,1,0:T(8,128)(2,1)S(1)} all-to-all(bf16[16,40,128]{2,1,0:T(8,128)(2,1)S(1)} %ensemble.2), channel_id=1, replica_groups=mesh['lev'=32,'mem'=16] {'mem'}, dimensions={0} | all-to-all | bytes 327680 | tf_op jit(solution)/shard_map/all_to_all | solution.py:413
  59.2 0.2 gradient.2
  59.4 11.1 %all_to_all.41.recv_ref.grad_ref = bf16[16,40,128]{2,1,0:T(8,128)(2,1)S(1)} all-to-all(bf16[16,40,128]{2,1,0:T(8,128)(2,1)S(1)} %gradient.2), channel_id=1, replica_groups=mesh['lev'=32,'mem'=16] {'mem'}, dimensions={0} | all-to-all | bytes 327680 | tf_op jit(solution)/shard_map/all_to_all | solution.py:413
  70.5 0.4 backward.2
  70.9 29.6 %all_to_all.42.recv_ref = bf16[32,40,128]{2,1,0:T(8,128)(2,1)S(1)} all-to-all(bf16[32,40,128]{2,1,0:T(8,128)(2,1)S(1)} %backward.2), channel_id=1, replica_groups=mesh['lev'=32,'mem'=16] {'lev'}, dimensions={0} | all-to-all | bytes 655360 | tf_op jit(solution)/shard_map/all_to_all | solution.py:413
  100.5 3.5 %backward_forward.1 = (bf16[32,40,128]{2,1,0:T(8,128)(2,1)S(1)}, bf16[32,40,128]{2,1,0:T(8,128)(2,1)}, bf16[5,128,128]{2,1,0:T(8,128)(2,1)}) custom-call(bf16[32,40,128]{2,1,0:T(8,128)(2,1)S(1)} %all_to_all.42.recv_ref, bf16[32,40,128]{2,1,0:T(8,128)(2,1)S(1)} %copy-done.3, bf16[256,64]{1,0:T(8,128)(2,1)S(1)} %fusion.3.pick_t_ref, ...), custom_call_target="tpu_custom_call" | custom-call | tf_op jit(solution)/shard_map/backward_forward/pallas_call | solution.py:36
  104.0 22.2 %all_to_all.43.recv_ref = bf16[32,40,128]{2,1,0:T(8,128)(2,1)S(1)} all-to-all(bf16[32,40,128]{2,1,0:T(8,128)(2,1)S(1)} %get-tuple-element.33), channel_id=1, replica_groups=mesh['lev'=32,'mem'=16] {'lev'}, dimensions={0} | all-to-all | bytes 655360 | tf_op jit(solution)/shard_map/all_to_all | solution.py:413
  126.3 0.3 ensemble.3
  126.6 11.3 %all_to_all.44.recv_ref = bf16[16,40,128]{2,1,0:T(8,128)(2,1)S(1)} all-to-all(bf16[16,40,128]{2,1,0:T(8,128)(2,1)S(1)} %ensemble.3), channel_id=1, replica_groups=mesh['lev'=32,'mem'=16] {'mem'}, dimensions={0} | all-to-all | bytes 327680 | tf_op jit(solution)/shard_map/all_to_all | solution.py:413
  137.8 0.2 gradient.3
  138.0 11.1 %all_to_all.45.recv_ref.grad_ref = bf16[16,40,128]{2,1,0:T(8,128)(2,1)S(1)} all-to-all(bf16[16,40,128]{2,1,0:T(8,128)(2,1)S(1)} %gradient.3), channel_id=1, replica_groups=mesh['lev'=32,'mem'=16] {'mem'}, dimensions={0} | all-to-all | bytes 327680 | tf_op jit(solution)/shard_map/all_to_all | solution.py:413
  149.1 0.4 backward.3
  149.5 28.2 %all_to_all.46.recv_ref = bf16[32,40,128]{2,1,0:T(8,128)(2,1)S(1)} all-to-all(bf16[32,40,128]{2,1,0:T(8,128)(2,1)S(1)} %backward.3), channel_id=1, replica_groups=mesh['lev'=32,'mem'=16] {'lev'}, dimensions={0} | all-to-all | bytes 655360 | tf_op jit(solution)/shard_map/all_to_all | solution.py:413
  177.7 2.9 %backward_last.1 = (bf16[2,5,4,4096]{3,2,1,0:T(4,128)(2,1)}, bf16[5,128,128]{2,1,0:T(8,128)(2,1)}) custom-call(bf16[32,40,128]{2,1,0:T(8,128)(2,1)S(1)} %all_to_all.46.recv_ref, bf16[32,40,128]{2,1,0:T(8,128)(2,1)S(1)} %copy-done.4, bf16[256,64]{1,0:T(8,128)(2,1)S(1)} %fusion.3.pick_t_ref, bf16[512,128]{1,0:T(8,128)(2,1)S(1)} %bitcast.33, ...), custom_call_target="tpu_custom_call" | custom-call | tf_op jit(solution)/shard_map/backward_last/pallas_call | solution.py:36
  (28 shorter events, 0.4 us)
Async XLA Ops:
  3.9 18.4 %copy-start.11 = (bf16[5,128,128]{2,1,0:T(8,128)(2,1)S(1)}, bf16[5,128,128]{2,1,0:T(8,128)(2,1)}, u32[]{:S(2)}) copy-start(bf16[5,128,128]{2,1,0:T(8,128)(2,1)} %param.16) | copy-start | bytes 491524
  3.9 40.4 %all-to-all-start = ((bf16[32,40,128]{2,1,0:T(8,128)(2,1)}), bf16[32,40,128]{2,1,0:T(8,128)(2,1)S(1)}, u32[]{:S(2)}, u32[]{:S(2)}) async-start(bf16[32,40,128]{2,1,0:T(8,128)(2,1)} %get-tuple-element.19), calls=%async_computation | async-start | bytes 655360 | tf_op jit(solution)/shard_map/all_to_all | solution.py:413
  20.8 0.7 copy-start.12
  22.5 0.9 copy-start.10
  23.4 0.8 copy-start.9
  24.3 20.0 %copy-start = (bf16[2,5,128,128]{3,2,1,0:T(8,128)(2,1)S(1)}, bf16[2,5,128,128]{3,2,1,0:T(8,128)(2,1)}, u32[]{:S(2)}) copy-start(bf16[2,5,128,128]{3,2,1,0:T(8,128)(2,1)} %perturb_ref.7) | copy-start | bytes 983044
  24.5 0.7 copy-start.6
  24.5 0.7 copy-start.7
  24.5 0.7 copy-start.8
  24.6 0.7 copy-start.5
  44.6 14.6 %copy-start.1 = (bf16[5,128,128]{2,1,0:T(8,128)(2,1)S(1)}, bf16[5,128,128]{2,1,0:T(8,128)(2,1)}, u32[]{:S(2)}) copy-start(bf16[5,128,128]{2,1,0:T(8,128)(2,1)} %static_ref.3) | copy-start | bytes 491524
  70.9 29.6 %copy-start.3 = (bf16[32,40,128]{2,1,0:T(8,128)(2,1)S(1)}, bf16[32,40,128]{2,1,0:T(8,128)(2,1)}, u32[]{:S(2)}) copy-start(bf16[32,40,128]{2,1,0:T(8,128)(2,1)} %get-tuple-element.27.kept_ref) | copy-start | bytes 983044
  126.6 11.3 %copy-start.2 = (bf16[5,128,128]{2,1,0:T(8,128)(2,1)S(1)}, bf16[5,128,128]{2,1,0:T(8,128)(2,1)}, u32[]{:S(2)}) copy-start(bf16[5,128,128]{2,1,0:T(8,128)(2,1)} %get-tuple-element.34.static_ref) | copy-start | bytes 491524
  149.5 28.2 %copy-start.4 = (bf16[32,40,128]{2,1,0:T(8,128)(2,1)S(1)}, bf16[32,40,128]{2,1,0:T(8,128)(2,1)}, u32[]{:S(2)}) copy-start(bf16[32,40,128]{2,1,0:T(8,128)(2,1)} %get-tuple-element.35.kept_ref) | copy-start | bytes 983044

commit v6 on v4

--- a/solution.py
+++ b/solution.py
@@ -21,6 +21,7 @@
 HALF = 64
 PAIRS = 32
 BLOCKS = 64
+STAGGER_NS = 6200
 GROUP = 5
 
 
@@ -192,28 +193,20 @@
     kept_ref,
     pick_t_ref,
     weight_t_ref,
-    grad_ref,
-    root_ref,
-    static_ref,
     source_hbm,
     weight_ref,
     send_ref,
     next_hbm,
-    moving_hbm,
     flat,
     moved,
     next_ref,
-    moving_ref,
     halves,
     moved_ahead,
     source_ref,
     sems,
 ):
-    fetch = pltpu.make_async_copy(source_hbm, source_ref, sems.at[2])
+    fetch = pltpu.make_async_copy(source_hbm, source_ref, sems.at[0])
     fetch.start()
-    descend_static(grad_ref, root_ref, static_ref, moving_ref)
-    keep_static = pltpu.make_async_copy(moving_ref, moving_hbm, sems.at[0])
-    keep_static.start()
     rows = recv_ref.shape[1]
     load, store = by_row(flat, rows)
     open_chunks(recv_ref, flat)
@@ -228,7 +221,6 @@
     keep = pltpu.make_async_copy(next_ref, next_hbm, sems.at[1])
     fetch.wait()
     gather(update, keep.start, lambda k, b: source_ref[k, b], send_ref, weight_ref, halves, moved_ahead)
-    keep_static.wait()
     keep.wait()
 
 
@@ -330,6 +322,15 @@
         send_ref[d] = grad
 
 
+def backward_hold(recv_ref, perturb_ref, vert_ref, root_ref, static_ref, send_ref, next_ref, flat, *, gain, hold):
+    backward(recv_ref, perturb_ref, vert_ref, send_ref, flat, gain=gain)
+    descend_static(recv_ref, root_ref, static_ref, next_ref)
+
+    @pl.when((lax.axis_index("mem") & 1) == 0)
+    def _():
+        pl.delay(hold)
+
+
 def backward(recv_ref, perturb_ref, vert_ref, send_ref, flat, *, gain):
     members, variables = perturb_ref.shape[:2]
     rows = send_ref.shape[1]
@@ -440,27 +441,34 @@
             gradient, parts, (), (across(partial, "mem"), static, own_root, slope, shift), gain=gain
         )
         grad = across(grad, "mem")
-        send = call(backward, chunks, (flat,), (grad, perturb, turned), gain=gain)
-        operands = (across(send, "lev"), held, pick_t, weight_t, grad, root_t, static)
         if turn + 1 < ITERS:
-            send, held, static = call(
+            send, static = call(
+                backward_hold,
+                (chunks, vmem(static.shape, BF16)),
+                (flat,),
+                (grad, perturb, turned, root_t, static),
+                gain=gain,
+                hold=STAGGER_NS,
+            )
+            send, held = call(
                 backward_forward,
-                (chunks, hbm(kept, BF16), hbm(static.shape, BF16)),
+                (chunks, hbm(kept, BF16)),
                 (
                     flat,
                     moved,
                     vmem(kept, BF16),
-                    vmem(static.shape, BF16),
                     halves,
                     moved_ahead,
                     pltpu.SMEM((slots, BLOCKS), jnp.int32),
-                    dma((3,)),
+                    dma((2,)),
                 ),
-                (*operands, source, weight),
-                stay=(7,),
+                (across(send, "lev"), held, pick_t, weight_t, source, weight),
+                stay=(4,),
             )
             recv = across(send, "lev")
         else:
+            send = call(backward, chunks, (flat,), (grad, perturb, turned), gain=gain)
+            operands = (across(send, "lev"), held, pick_t, weight_t, grad, root_t, static)
             control, static = call(
                 backward_last,
                 (hbm(control.shape, BF16), hbm(static.shape, BF16)),

time: 186 us -> 181 us (0.973)
  blocking collectives: 133 us -> 128 us
    all_to_all x7, blocking collectives: 133 us -> 128 us  [on_device(): across = lambda x, axis: lax.all_to_all(x, axis, 0, 0, tiled=True)]
where the time goes in v6:
time: 181 us; the launch traced here: 180 us
  blocking collectives  128 us (71%)
  waiting for transfers between devices  18.1 us (10%)
  starting transfers between devices  16.9 us (9%)
  Pallas kernels  12 us (7%)
  local copies, waits for them, and re-layouts  3.77 us (2%)
    all_to_all x7, blocking collectives, on_device(): across = lambda x, axis: lax.all_to_all(x, axis, 0, 0, tiled=True)  128 us
    all_to_all x1, waiting for transfers between devices, on_device(): across = lambda x, axis: lax.all_to_all(x, axis, 0, 0, tiled=True)  18.1 us
    all_to_all x1, starting transfers between devices, on_device(): across = lambda x, axis: lax.all_to_all(x, axis, 0, 0, tiled=True)  16.9 us
    pallas_call x10, Pallas kernels, call(): run(*(a if i in stay else pltpu.with_memory_space_constraint(a, pltpu.VME...  12 us
  transfers between devices with their start and end apart: 1, of which 1 were waited for; matrix products, arithmetic and copies ran while one was open for 1% of the time, Pallas kernels for 0%

profile of v6, /device:TPU:2, one launch (start us, length us, event | category | flops | bytes accessed | tf_op | source)
XLA Modules:
  0.0 180.3 jit_solution(9694344237132396632)
XLA Ops:
  0.6 3.3 %forward_first.1 = (bf16[32,40,128]{2,1,0:T(8,128)(2,1)}, bf16[32,40,128]{2,1,0:T(8,128)(2,1)}) custom-call(bf16[2,5,4,4096]{3,2,1,0:T(4,128)(2,1)} %control_hbm.1, s32[4,64]{1,0:T(4,128)} %bitcast.42, bf16[4,64,64]{2,1,0:T(8,128)(2,1)} %tiles_hbm.1), custom_call_target="tpu_custom_call" | custom-call | tf_op jit(solution)/shard_map/forward_first/pallas_call | solution.py:36
  3.9 16.9 %all-to-all-start = ((bf16[32,40,128]{2,1,0:T(8,128)(2,1)}), bf16[32,40,128]{2,1,0:T(8,128)(2,1)S(1)}, u32[]{:S(2)}, u32[]{:S(2)}) async-start(bf16[32,40,128]{2,1,0:T(8,128)(2,1)} %get-tuple-element.20), calls=%async_computation | async-start | bytes 655360 | tf_op jit(solution)/shard_map/all_to_all | solution.py:408
  20.9 0.6 copy-done.11
  21.5 0.6 fusion.6
  22.1 0.1 copy.19
  22.1 0.1 copy.20
  22.3 0.2 copy.17
  22.5 0.9 copy-done.9
  23.4 0.2 copy.16
  23.6 0.7 copy-done.8
  24.4 0.1 copy.21
  24.6 0.1 fusion.3.pick_t_ref
  24.7 0.5 copy-done.5
  25.2 0.1 copy-done.4
  25.4 0.7 observations.1
  26.1 0.1 fusion.2
  26.2 18.1 %all-to-all-done.recv_ref = bf16[32,40,128]{2,1,0:T(8,128)(2,1)S(1)} async-done(((bf16[32,40,128]{2,1,0:T(8,128)(2,1)}), bf16[32,40,128]{2,1,0:T(8,128)(2,1)S(1)}, u32[]{:S(2)}, u32[]{:S(2)}) %all-to-all-start) | async-done | bytes 327712 | tf_op jit(solution)/shard_map/all_to_all | solution.py:408
  44.3 0.3 ensemble.2
  44.6 14.6 %all_to_all.40.recv_ref = bf16[16,40,128]{2,1,0:T(8,128)(2,1)S(1)} all-to-all(bf16[16,40,128]{2,1,0:T(8,128)(2,1)S(1)} %ensemble.2), channel_id=1, replica_groups=mesh['lev'=32,'mem'=16] {'mem'}, dimensions={0} | all-to-all | bytes 327680 | tf_op jit(solution)/shard_map/all_to_all | solution.py:408
  59.2 0.2 gradient.2
  59.4 11.1 %all_to_all.41.recv_ref = bf16[16,40,128]{2,1,0:T(8,128)(2,1)S(1)} all-to-all(bf16[16,40,128]{2,1,0:T(8,128)(2,1)S(1)} %gradient.2), channel_id=1, replica_groups=mesh['lev'=32,'mem'=16] {'mem'}, dimensions={0} | all-to-all | bytes 327680 | tf_op jit(solution)/shard_map/all_to_all | solution.py:408
  70.5 0.4 backward_hold.1
  71.0 29.3 %all_to_all.42.recv_ref = bf16[32,40,128]{2,1,0:T(8,128)(2,1)S(1)} all-to-all(bf16[32,40,128]{2,1,0:T(8,128)(2,1)S(1)} %get-tuple-element.29), channel_id=1, replica_groups=mesh['lev'=32,'mem'=16] {'lev'}, dimensions={0} | all-to-all | bytes 655360 | tf_op jit(solution)/shard_map/all_to_all | solution.py:408
  100.3 3.4 %backward_forward.1 = (bf16[32,40,128]{2,1,0:T(8,128)(2,1)S(1)}, bf16[32,40,128]{2,1,0:T(8,128)(2,1)}) custom-call(bf16[32,40,128]{2,1,0:T(8,128)(2,1)S(1)} %all_to_all.42.recv_ref, bf16[32,40,128]{2,1,0:T(8,128)(2,1)S(1)} %copy-done.2, bf16[256,64]{1,0:T(8,128)(2,1)S(1)} %fusion.3.pick_t_ref, bf16[512,128]{1,0:T(8,128)(2,1)S(1)} %bitcast.32, ...), custom_call_target="tpu_custom_call" | custom-call | tf_op jit(solution)/shard_map/backward_forward/pallas_call | solution.py:36
  103.7 22.1 %all_to_all.43.recv_ref = bf16[32,40,128]{2,1,0:T(8,128)(2,1)S(1)} all-to-all(bf16[32,40,128]{2,1,0:T(8,128)(2,1)S(1)} %get-tuple-element.35), channel_id=1, replica_groups=mesh['lev'=32,'mem'=16] {'lev'}, dimensions={0} | all-to-all | bytes 655360 | tf_op jit(solution)/shard_map/all_to_all | solution.py:408
  125.8 0.3 ensemble.3
  126.1 11.5 %all_to_all.44.recv_ref = bf16[16,40,128]{2,1,0:T(8,128)(2,1)S(1)} all-to-all(bf16[16,40,128]{2,1,0:T(8,128)(2,1)S(1)} %ensemble.3), channel_id=1, replica_groups=mesh['lev'=32,'mem'=16] {'mem'}, dimensions={0} | all-to-all | bytes 327680 | tf_op jit(solution)/shard_map/all_to_all | solution.py:408
  137.6 0.2 gradient.3
  137.7 11.1 %all_to_all.45.recv_ref.grad_ref = bf16[16,40,128]{2,1,0:T(8,128)(2,1)S(1)} all-to-all(bf16[16,40,128]{2,1,0:T(8,128)(2,1)S(1)} %gradient.3), channel_id=1, replica_groups=mesh['lev'=32,'mem'=16] {'mem'}, dimensions={0} | all-to-all | bytes 327680 | tf_op jit(solution)/shard_map/all_to_all | solution.py:408
  148.8 0.4 backward.1
  149.2 28.1 %all_to_all.46.recv_ref = bf16[32,40,128]{2,1,0:T(8,128)(2,1)S(1)} all-to-all(bf16[32,40,128]{2,1,0:T(8,128)(2,1)S(1)} %backward.1), channel_id=1, replica_groups=mesh['lev'=32,'mem'=16] {'lev'}, dimensions={0} | all-to-all | bytes 655360 | tf_op jit(solution)/shard_map/all_to_all | solution.py:408
  177.4 2.9 %backward_last.1 = (bf16[2,5,4,4096]{3,2,1,0:T(4,128)(2,1)}, bf16[5,128,128]{2,1,0:T(8,128)(2,1)}) custom-call(bf16[32,40,128]{2,1,0:T(8,128)(2,1)S(1)} %all_to_all.46.recv_ref, bf16[32,40,128]{2,1,0:T(8,128)(2,1)S(1)} %copy-done.3, bf16[256,64]{1,0:T(8,128)(2,1)S(1)} %fusion.3.pick_t_ref, bf16[512,128]{1,0:T(8,128)(2,1)S(1)} %bitcast.33, ...), custom_call_target="tpu_custom_call" | custom-call | tf_op jit(solution)/shard_map/backward_last/pallas_call | solution.py:36
  (26 shorter events, 0.4 us)
Async XLA Ops:
  3.9 18.4 %copy-start.10 = (bf16[5,128,128]{2,1,0:T(8,128)(2,1)S(1)}, bf16[5,128,128]{2,1,0:T(8,128)(2,1)}, u32[]{:S(2)}) copy-start(bf16[5,128,128]{2,1,0:T(8,128)(2,1)} %param.16) | copy-start | bytes 491524
  3.9 40.4 %all-to-all-start = ((bf16[32,40,128]{2,1,0:T(8,128)(2,1)}), bf16[32,40,128]{2,1,0:T(8,128)(2,1)S(1)}, u32[]{:S(2)}, u32[]{:S(2)}) async-start(bf16[32,40,128]{2,1,0:T(8,128)(2,1)} %get-tuple-element.20), calls=%async_computation | async-start | bytes 655360 | tf_op jit(solution)/shard_map/all_to_all | solution.py:408
  20.8 0.7 copy-start.11
  22.5 0.9 copy-start.9
  23.4 0.8 copy-start.8
  24.4 19.9 %copy-start = (bf16[2,5,128,128]{3,2,1,0:T(8,128)(2,1)S(1)}, bf16[2,5,128,128]{3,2,1,0:T(8,128)(2,1)}, u32[]{:S(2)}) copy-start(bf16[2,5,128,128]{3,2,1,0:T(8,128)(2,1)} %perturb_ref.7) | copy-start | bytes 983044
  24.5 0.7 copy-start.5
  24.5 0.7 copy-start.6
  24.5 0.7 copy-start.7
  24.7 0.7 copy-start.4
  44.6 14.6 %copy-start.1 = (bf16[5,128,128]{2,1,0:T(8,128)(2,1)S(1)}, bf16[5,128,128]{2,1,0:T(8,128)(2,1)}, u32[]{:S(2)}) copy-start(bf16[5,128,128]{2,1,0:T(8,128)(2,1)} %static_ref.3) | copy-start | bytes 491524
  71.0 29.3 %copy-start.2 = (bf16[32,40,128]{2,1,0:T(8,128)(2,1)S(1)}, bf16[32,40,128]{2,1,0:T(8,128)(2,1)}, u32[]{:S(2)}) copy-start(bf16[32,40,128]{2,1,0:T(8,128)(2,1)} %get-tuple-element.30.kept_ref) | copy-start | bytes 983044
  149.2 28.1 %copy-start.3 = (bf16[32,40,128]{2,1,0:T(8,128)(2,1)S(1)}, bf16[32,40,128]{2,1,0:T(8,128)(2,1)}, u32[]{:S(2)}) copy-start(bf16[32,40,128]{2,1,0:T(8,128)(2,1)} %get-tuple-element.37.kept_ref) | copy-start | bytes 983044
